TPU v7x, 32 devices: a whole 2x2x4 slice. The times are simulated.
32 devices in a mesh: group: 8 (over z, x), dom: 4 (over y, core).
Axes of the slice: x: 2, y: 2, z: 4, core: 2. Of those that a mesh axis runs over, the one named last changes fastest.
Arguments:
- features: bfloat16 [65536, 128], P(('group', 'dom')), may hold values from -6 to 6
- w_in: bfloat16 [128, 1024], replicated, may hold values from -0.5 to 0.5
- b_in: float32 [1024], replicated, may hold values from -4 to 4
- w_out: bfloat16 [1024, 128], replicated, may hold values from -0.1875 to 0.1875
- anchor_ids: int32 [131072], P(('group', 'dom')), may hold values from 0 to 8191
- local_tiles: int32 [1024, 4], P(('group', 'dom')), may hold values from 0 to 63
- requests: int32 [8, 4, 8, 8], P('group', 'dom'), may hold values from 0 to 63
- counts: int32 [8, 4, 8], P('group', 'dom'), may hold values from 0 to 8, as said below
- remote_refs: int32 [1024, 4], P(('group', 'dom')), may hold values from 0 to 63
- teacher: bfloat16 [131072, 1024], P(('group', 'dom')), may hold values from -12 to 12
Outputs:
- anchor_kl: float32 [131072], P(('group', 'dom'))
- node_grad: float32 [65536, 128], P(('group', 'dom'))
- grad_w_in: float32 [128, 1024], replicated
- grad_b_in: float32 [1024], replicated
- grad_w_out: float32 [1024, 128], replicated
Inputs may be any that keep to these rules, and one draw needn't show every extreme that they name: `requests`: slots at or past the count hold tile numbers too. counts[g, d, g] is 0; in every draw some device has 8 live slots from every other group.
All inputs are finite; a program needn't handle non-finite values.
Results may differ from a plain program's by a relative error of at most 0.0067.
Values may be sent and summed in bfloat16 or wider, within the bound.
A program may use at most 192 MiB of HBM per device.

v0:
```python
import math

import jax
import jax.numpy as jnp
from jax import lax
from jax.sharding import PartitionSpec as P

TILE = 128
ABLK = 128


SCORE_SCALE = 8.0
EPSILON = 1e-06


def node_forward(feature_rows, w_in, b_in, w_out):
    pre_act = jnp.dot(feature_rows, w_in, preferred_element_type=jnp.float32) + b_in
    hidden = jax.nn.silu(pre_act).astype(jnp.bfloat16)
    embedding = jnp.dot(hidden, w_out, preferred_element_type=jnp.float32)
    spread = jnp.sqrt(jnp.mean(embedding * embedding, axis=1, keepdims=True) + EPSILON)
    unit_rows = (embedding / spread).astype(jnp.bfloat16)
    return (pre_act, hidden, embedding, spread, unit_rows)


def shards(
    features, w_in, b_in, w_out, anchor_ids, local_tiles, requests, counts, remote_refs, teacher
):
    groups = lax.axis_size("group")
    devices = groups * lax.axis_size("dom")
    emb_width = w_out.shape[1]
    pre_act, hidden, embedding, spread, unit_rows = node_forward(features, w_in, b_in, w_out)
    group_unit = lax.all_gather(unit_rows, "dom", axis=0, tiled=True)
    group_rows = group_unit.shape[0]
    group_tiles = group_rows // TILE
    tile_table = group_unit.reshape(group_tiles, TILE, emb_width)
    own_requests = requests[0, 0]
    own_counts = counts[0, 0]
    slot_count = own_requests.shape[1]
    asked = lax.all_to_all(own_requests, "group", split_axis=0, concat_axis=0, tiled=True)
    fetched = lax.all_to_all(tile_table[asked], "group", split_axis=0, concat_axis=0, tiled=True)
    context_table = jnp.concatenate(
        [tile_table, fetched.reshape(groups * slot_count, TILE, emb_width)], axis=0
    )
    table_tiles = context_table.shape[0]
    table_rows = context_table.reshape(-1, emb_width)
    table_flat = context_table.reshape(table_tiles, TILE * emb_width)
    table_iota = jnp.arange(table_tiles, dtype=jnp.int32)
    slot_live = (jnp.arange(slot_count, dtype=jnp.int32)[None, :] < own_counts[:, None]).reshape(-1)
    tile_live = jnp.concatenate([jnp.ones((group_tiles,), jnp.bool_), slot_live]).astype(
        jnp.float32
    )
    block_count = local_tiles.shape[0]
    per_step = math.gcd(block_count, 4)
    step_count = block_count // per_step
    context_width = teacher.shape[1]
    tiles_each = local_tiles.shape[1] + remote_refs.shape[1]
    anchor_steps = anchor_ids.reshape(step_count, per_step, ABLK)
    all_tiles = jnp.concatenate([local_tiles, remote_refs + group_tiles], axis=1)
    tile_steps = all_tiles.reshape(step_count, per_step, tiles_each)
    teacher_steps = teacher.reshape(step_count, per_step, ABLK, context_width)
    score_scale = SCORE_SCALE / emb_width

    def score_block(carry, inputs):
        anchor_block, tile_block, teacher_block = inputs
        anchor_vecs = table_rows[anchor_block]
        pick = (tile_block.reshape(-1)[:, None] == table_iota[None, :]).astype(jnp.bfloat16)
        context_flat = jnp.dot(pick, table_flat, preferred_element_type=jnp.float32).astype(
            jnp.bfloat16
        )
        context_vecs = context_flat.reshape(per_step, context_width, emb_width)
        live_mask = jnp.repeat(tile_live[tile_block], TILE, axis=1)[:, None, :]
        scores = (
            jnp.einsum(
                "bae,bce->bac", anchor_vecs, context_vecs, preferred_element_type=jnp.float32
            )
            * score_scale
        )
        student_exp = jnp.exp(scores) * live_mask
        student_total = jnp.sum(student_exp, axis=2, keepdims=True)
        teacher_f = teacher_block.astype(jnp.float32)
        target_exp = jnp.exp(teacher_f) * live_mask
        target_total = jnp.sum(target_exp, axis=2, keepdims=True)
        target_prob = target_exp / target_total
        divergence = (
            jnp.sum(target_prob * (teacher_f - scores), axis=2)
            - jnp.log(target_total[:, :, 0])
            + jnp.log(student_total[:, :, 0])
        )
        prob_delta = (student_exp / student_total - target_prob).astype(jnp.bfloat16)
        anchor_grad = (
            jnp.einsum("bac,bce->bae", prob_delta, context_vecs, preferred_element_type=jnp.float32)
            * score_scale
        )
        context_grad = (
            jnp.einsum("bac,bae->bce", prob_delta, anchor_vecs, preferred_element_type=jnp.float32)
            * score_scale
        )
        return (
            carry,
            (
                divergence,
                anchor_grad,
                context_grad.reshape(per_step * tiles_each, TILE * emb_width),
            ),
        )

    unused, outputs = lax.scan(
        score_block, jnp.zeros((), jnp.float32), (anchor_steps, tile_steps, teacher_steps)
    )
    divergence, anchor_grads, context_grads = outputs
    anchor_kl = divergence.reshape(-1)
    context_flat_grads = context_grads.reshape(-1, TILE * emb_width)
    high_part = context_flat_grads.astype(jnp.bfloat16)
    low_part = (context_flat_grads - high_part.astype(jnp.float32)).astype(jnp.bfloat16)
    placing = (all_tiles.reshape(-1)[:, None] == table_iota[None, :]).astype(jnp.bfloat16)
    contract = (((0,), (0,)), ((), ()))
    tile_sums = lax.dot_general(placing, high_part, contract, preferred_element_type=jnp.float32)
    tile_sums = tile_sums + lax.dot_general(
        placing, low_part, contract, preferred_element_type=jnp.float32
    )
    grad_rows = (
        tile_sums.reshape(-1, emb_width).at[anchor_ids].add(anchor_grads.reshape(-1, emb_width))
    )
    local_grad = grad_rows[:group_rows]
    remote_grad = grad_rows[group_rows:].reshape(groups, slot_count, TILE, emb_width)
    returned = lax.all_to_all(
        remote_grad.astype(jnp.bfloat16), "group", split_axis=0, concat_axis=0, tiled=True
    ).astype(remote_grad.dtype)
    returned_tiles = returned.reshape(-1, TILE, emb_width)
    asked_flat = asked.reshape(-1)
    context_part = lax.psum_scatter(local_grad, "dom", scatter_dimension=0, tiled=True)
    returned_rows = (
        jnp.zeros((group_tiles, TILE, emb_width), jnp.float32)
        .at[asked_flat]
        .add(returned_tiles)
        .reshape(group_rows, emb_width)
    )
    returned_part = lax.psum_scatter(
        returned_rows.astype(jnp.bfloat16), "dom", scatter_dimension=0, tiled=True
    ).astype(jnp.float32)
    node_grad = context_part + returned_part
    normed = embedding / spread
    embed_grad = (
        (node_grad - normed * jnp.mean(node_grad * normed, axis=1, keepdims=True)) / spread
    ).astype(jnp.bfloat16)
    out_grad = jnp.dot(hidden.T, embed_grad, preferred_element_type=jnp.float32)
    hidden_grad = jnp.dot(embed_grad, w_out.T, preferred_element_type=jnp.float32)
    sigmoid_pre = jax.nn.sigmoid(pre_act)
    pre_grad = hidden_grad * sigmoid_pre * (1.0 + pre_act * (1.0 - sigmoid_pre))
    bias_grad = jnp.sum(pre_grad, axis=0)
    in_grad = jnp.dot(features.T, pre_grad.astype(jnp.bfloat16), preferred_element_type=jnp.float32)
    totals = lax.psum((in_grad, bias_grad, out_grad), ("group", "dom"))
    inverse = 1.0 / devices
    return (anchor_kl, node_grad, totals[0] * inverse, totals[1] * inverse, totals[2] * inverse)


def solution(mesh):
    return jax.shard_map(
        shards,
        mesh=mesh,
        in_specs=(
            P(("group", "dom"), None),
            P(),
            P(),
            P(),
            P(("group", "dom")),
            P(("group", "dom"), None),
            P("group", "dom", None, None),
            P("group", "dom", None),
            P(("group", "dom"), None),
            P(("group", "dom"), None),
        ),
        out_specs=(P(("group", "dom")), P(("group", "dom"), None), P(), P(), P()),
        check_vma=False,
    )
```

profile of v0, /device:TPU:1, one launch (start us, length us, event | category | flops | bytes accessed | tf_op | source)
XLA Modules:
  0.0 651.4 jit_solution(16230016798141399763)
XLA Ops:
  8.2 5.3 multiply_convert_fusion
  18.9 11.5 %all_to_all.22 = s32[8,1,8]{2,1,0:T(1,128)S(1)} all-to-all(s32[8,1,8]{2,1,0:T(1,128)S(1)} %bitcast.138), channel_id=1, replica_groups=mesh['group'=8,'dom'=4] {'group'}, dimensions={0} | all-to-all | bytes 512 | tf_op jit(solution)/shard_map/all_to_all | solution.py:39
  30.5 13.6 %all-gather.2.cloned.1.call-done = bf16[8192,128]{0,1:T(8,128)(2,1)} async-done(((bf16[2048,128]{0,1:T(8,128)(2,1)}), bf16[8192,128]{0,1:T(8,128)(2,1)}) %all-gather.2.cloned.1.call-update) | async-done | bytes 2097168 | tf_op jit(solution)/shard_map/all_gather | solution.py:32
  46.4 2.9 copy.37
  49.3 3.8 gather_fusion.2
  53.1 5.2 all-to-all-start.1
  58.8 4.1 copy.40
  62.9 4.2 concatenate.19
  67.1 39.0 %all-to-all-done.1 = bf16[8,8,128,128]{3,2,1,0:T(8,128)(2,1)S(1)} async-done(((bf16[8,8,128,128]{3,2,1,0:T(8,128)(2,1)}), bf16[8,8,128,128]{3,2,1,0:T(8,128)(2,1)S(1)}, u32[]{:S(2)}, u32[]{:S(2)}) %all-to-all-start.1) | async-done | bytes 2097184 | tf_op jit(solution)/shard_map/all_to_all | solution.py:40
  106.1 2.8 copy.38
  108.9 4.8 pad_maximum_fusion
  113.7 6.9 %copy.39 = bf16[128,128,128]{2,1,0:T(8,128)(2,1)} copy(bf16[128,128,128]{1,0,2:T(8,128)(2,1)} %pad_maximum_fusion) | data formatting | bytes 8388608 | tf_op jit(solution)/shard_map/concatenate | solution.py:41
  124.6 166.6 %while.15 = (s32[]{:T(128)}, f32[8,4,128]{2,1,0:T(4,128)S(1)}, f32[8,4,128,128]{3,2,1,0:T(8,128)}, f32[8,32,16384]{2,1,0:T(8,128)}, bf16[8,4,128,1024]{3,2,1,0:T...) while((s32[]{:T(128)}, f32[8,4,128]{2,1,0:T(4,128)S(1)}, ...), condition=%wide.region_5.6_spmd.clone, body=%wide.region_1.5_spmd.clone.sunk | while | flops 548478080 | bytes 31332372 | solution.py:107
  127.3 3.8 gather_fusion.1
  131.2 2.9 convolution_convert_fusion.2
  148.1 3.8 gather_fusion.1
  152.0 2.9 convolution_convert_fusion.2
  168.9 3.8 gather_fusion.1
  172.8 2.9 convolution_convert_fusion.2
  189.7 3.8 gather_fusion.1
  193.6 2.9 convolution_convert_fusion.2
  210.6 3.8 gather_fusion.1
  214.5 2.9 convolution_convert_fusion.2
  231.4 3.8 gather_fusion.1
  235.3 2.9 convolution_convert_fusion.2
  252.2 3.8 gather_fusion.1
  256.1 2.9 convolution_convert_fusion.2
  273.1 3.8 gather_fusion.1
  276.9 2.9 convolution_convert_fusion.2
  291.2 7.2 %fusion.12 = (bf16[256,16384]{1,0:T(8,128)(2,1)S(1)}, bf16[256,16384]{1,0:T(8,128)(2,1)S(1)}) fusion(f32[8,32,16384]{2,1,0:T(8,128)} %get-tuple-element.65), kind=kLoop, calls=%fused_computation.36 | loop fusion | flops 16777216 | bytes 33554432 | tf_op jit(solution)/shard_map/convert_element_type | solution.py:114
  299.8 4.7 convolution_add_fusion
  304.5 9.4 %reshape.244 = f32[16384,128]{1,0:T(8,128)} reshape(f32[128,16384]{1,0:T(8,128)} %convolution_add_fusion) | data formatting | bytes 16777216 | tf_op jit(solution)/shard_map/reshape | solution.py:122
  313.9 26.7 %scatter_fusion = f32[16384,128]{1,0:T(8,128)} fusion(f32[16384,128]{1,0:T(8,128)} %reshape.244, s32[4096]{0:T(1024)S(1)} %compare_select_fusion.2, f32[4096,128]{1,0:T(8,128)S(1)} %bitcast.134), kind=kCustom, calls=%fused_computation.3 | custom fusion | flops 524288 | bytes 6307840 | tf_op jit(solution)/shard_map/scatter-add | solution.py:122
  340.6 3.7 slice.18
  344.3 4.2 all-to-all-start.2
  349.8 46.2 %all-to-all-done.2 = bf16[8,8,128,128]{3,2,1,0:T(8,128)(2,1)S(1)} async-done(((bf16[8,8,128,128]{3,2,1,0:T(8,128)(2,1)}), bf16[8,8,128,128]{3,2,1,0:T(8,128)(2,1)S(1)}, u32[]{:S(2)}, u32[]{:S(2)}) %all-to-all-start.2) | async-done | bytes 2097184 | tf_op jit(solution)/shard_map/all_to_all | solution.py:126
  396.0 2.6 bitcast_convert_fusion.1
  398.6 2.5 broadcast_in_dim.45
  401.1 13.4 %scatter_fusion.1 = f32[64,128,128]{2,1,0:T(8,128)} fusion(f32[64,128,128]{2,1,0:T(8,128)} %broadcast_in_dim.45, s32[64]{0:T(128)S(1)} %fusion.21, f32[64,128,128]{2,1,0:T(8,128)} %bitcast_convert_fusion.1), kind=kCustom, calls=%fused_computation.4 | custom fusion | flops 1048576 | bytes 12583168 | tf_op jit(solution)/shard_map/scatter-add | solution.py:135
  414.5 2.6 convert_element_type.59
  417.1 2.9 copy.47
  420.1 4.4 slice.15
  424.5 6.1 copy.48
  430.7 20.3 %reduce-scatter.5.cloned.1.call-done = bf16[2048,128]{0,1:T(8,128)(2,1)} async-done(((bf16[8192,128]{0,1:T(8,128)(2,1)}), bf16[2048,128]{0,1:T(8,128)(2,1)}) %reduce-scatter.5.cloned.1.call-update) | async-done | bytes 524304 | tf_op jit(solution)/shard_map/reduce_scatter | solution.py:138
  451.0 47.2 %reduce-scatter.3.cloned.1.call-done = f32[2048,128]{0,1:T(8,128)} async-done(((f32[8192,128]{0,1:T(8,128)}), f32[2048,128]{0,1:T(8,128)}) %reduce-scatter.3.cloned.1.call-update) | async-done | bytes 1048592 | tf_op jit(solution)/shard_map/reduce_scatter | solution.py:131
  503.0 6.3 fusion.23
  512.7 39.1 %psum.22 = f32[1024]{0:T(1024)S(1)} all-reduce(f32[1024]{0:T(1024)S(1)} %get-tuple-element.139), channel_id=1, replica_groups=mesh['group'=8,'dom'=4] {'group','dom'}, use_global_device_ids=true, to_apply=%region_13.14 | all-reduce | flops 1024 | bytes 8192 | tf_op jit(solution)/shard_map/psum | solution.py:152
  552.4 88.5 %all-reduce.4.cloned.1.call-done = (f32[128,1024]{0,1:T(8,128)}, f32[1024,128]{1,0:T(8,128)}) async-done(((f32[128,1024]{0,1:T(8,128)}, f32[1024,128]{1,0:T(8,128)}), (f32[128,1024]{0,1:T(8,128)}, f32[1024,128]{1,0:T(8,128)})) %all-reduce.4.cloned.1.call-update) | async-done | bytes 1048592 | tf_op jit(solution)/shard_map/psum | solution.py:152
  (227 shorter events, 141.2 us)
Async XLA Ops:
  7.2 1.0 copy-start
  7.2 8.3 %copy-start.8 = (bf16[1024,128]{1,0:T(8,128)(2,1)S(1)}, bf16[1024,128]{1,0:T(8,128)(2,1)}, u32[]{:S(2)}) copy-start(bf16[1024,128]{1,0:T(8,128)(2,1)} %param.15) | copy-start | bytes 786436
  7.2 37.0 %all-gather.2.cloned.1.call-start = ((), (), s32[]{:S(2)}) async-start(), calls=%async_computation.5 | async-start | bytes 2621440 | tf_op jit(solution)/shard_map/all_gather | solution.py:32
  13.6 1.9 copy-start.1
  13.6 5.4 copy-start.10
  17.1 1.0 copy-start.4
  46.3 6.7 %copy-start.3 = (bf16[16,8,64,128]{3,2,1,0:T(8,128)(2,1)}, bf16[16,8,64,128]{3,2,1,0:T(8,128)(2,1)S(1)}, u32[]{:S(2)}) copy-start(bf16[16,8,64,128]{3,2,1,0:T(8,128)(2,1)S(1)} %copy.50) | copy-start | bytes 6291460
  49.3 9.0 %copy-start.11 = (s32[32,4]{0,1:T(4,128)S(1)}, s32[32,4]{0,1:T(4,128)}, u32[]{:S(2)}) copy-start(s32[32,4]{0,1:T(4,128)} %param.20) | copy-start | bytes 1540
  49.3 9.1 %copy-start.12 = (s32[32,4]{0,1:T(4,128)S(1)}, s32[32,4]{0,1:T(4,128)}, u32[]{:S(2)}) copy-start(s32[32,4]{0,1:T(4,128)} %param.17) | copy-start | bytes 1540
  49.3 9.2 %copy-start.15 = (s32[1,1,8]{2,1,0:T(1,128)S(1)}, s32[1,1,8]{2,1,0:T(1,128)}, u32[]{:S(2)}) copy-start(s32[1,1,8]{2,1,0:T(1,128)} %param.19) | copy-start | bytes 100
  49.3 9.5 %copy-start.9 = (s32[4096]{0:T(1024)S(1)}, s32[4096]{0:T(1024)}, u32[]{:S(2)}) copy-start(s32[4096]{0:T(1024)} %param.16) | copy-start | bytes 49156
  53.1 53.1 %all-to-all-start.1 = ((bf16[8,8,128,128]{3,2,1,0:T(8,128)(2,1)}), bf16[8,8,128,128]{3,2,1,0:T(8,128)(2,1)S(1)}, u32[]{:S(2)}, u32[]{:S(2)}) async-start(bf16[8,8,128,128]{3,2,1,0:T(8,128)(2,1)} %bitcast.126), calls=%async_computation.1 | async-start | bytes 4194304 | tf_op jit(solution)/shard_map/all_to_all | solution.py:40
  120.6 1.6 copy-start.6
  291.2 7.2 %copy-start.13 = (f32[8,4,128]{2,1,0:T(4,128)}, f32[8,4,128]{2,1,0:T(4,128)S(1)}, u32[]{:S(2)}) copy-start(f32[8,4,128]{2,1,0:T(4,128)S(1)} %get-tuple-element.64) | copy-start | bytes 49156
  304.5 9.4 %copy-start.7 = (f32[8,4,128,128]{3,2,1,0:T(8,128)S(1)}, f32[8,4,128,128]{3,2,1,0:T(8,128)}, u32[]{:S(2)}) copy-start(f32[8,4,128,128]{3,2,1,0:T(8,128)} %get-tuple-element.66) | copy-start | bytes 6291460
  344.3 51.7 %all-to-all-start.2 = ((bf16[8,8,128,128]{3,2,1,0:T(8,128)(2,1)}), bf16[8,8,128,128]{3,2,1,0:T(8,128)(2,1)S(1)}, u32[]{:S(2)}, u32[]{:S(2)}) async-start(bf16[8,8,128,128]{3,2,1,0:T(8,128)(2,1)} %bitcast.128), calls=%async_computation.3 | async-start | bytes 4194304 | tf_op jit(solution)/shard_map/all_to_all | solution.py:126
  348.5 102.5 %reduce-scatter.5.cloned.1.call-start = ((), (), s32[]{:S(2)}) async-start(), calls=%async_computation.7 | async-start | bytes 2621440 | tf_op jit(solution)/shard_map/reduce_scatter | solution.py:138
  420.1 78.2 %reduce-scatter.3.cloned.1.call-start = ((), (), s32[]{:S(2)}) async-start(), calls=%async_computation.6 | async-start | bytes 5242880 | tf_op jit(solution)/shard_map/reduce_scatter | solution.py:131
  430.7 67.6 %copy-start.5 = (f32[2048,128]{0,1:T(8,128)S(1)}, f32[2048,128]{0,1:T(8,128)}, u32[]{:S(2)}) copy-start(f32[2048,128]{0,1:T(8,128)} %copy-done.4) | copy-start | bytes 3145732
  430.7 210.2 %all-reduce.4.cloned.1.call-start = ((), (), s32[]{:S(2)}) async-start(), calls=%async_computation.8 | async-start | bytes 2097152 | tf_op jit(solution)/shard_map/psum | solution.py:152
  498.2 2.7 copy-start.2
  500.0 3.0 copy-start.14
Sparse Core Ops, SparseCore 0:
  19.1 25.0 all-gather.1
  420.2 30.7 reduce-scatter.4
  453.7 44.5 reduce-scatter.2
  511.5 129.3 all-reduce.3
where the time goes:
time: 656 us; the launch traced here: 651 us
  waiting for transfers between devices  255 us (39%)
  local copies, waits for them, and re-layouts  134 us (20%)
  other arithmetic  98 us (15%)
  matrix products  90 us (14%)
  blocking collectives  50.6 us (8%)
  between operations  14 us (2%)
  starting transfers between devices  9.56 us (1%)
    psum x1, waiting for transfers between devices, shards(): totals = lax.psum((in_grad, bias_grad, out_grad), ('group', 'dom'))  88.5 us
    reduce_scatter x1, waiting for transfers between devices, shards(): lax.psum_scatter(local_grad, 'dom', scatter_dimension=0, tiled=True)  47.2 us
    all_to_all x1, waiting for transfers between devices, shards(): lax.all_to_all(remote_grad.astype(jnp.bfloat16), 'group', split_axis=0, c...  46.2 us
    psum x1, blocking collectives, shards(): totals = lax.psum((in_grad, bias_grad, out_grad), ('group', 'dom'))  39.1 us
    all_to_all x1, waiting for transfers between devices, shards(): lax.all_to_all(tile_table[asked], 'group', split_axis=0, concat_axis=0, t...  39 us
    gather x8, local copies, waits for them, and re-layouts, score_block(): anchor_vecs = table_rows[anchor_block]  30.2 us
    scatter-add x1, other arithmetic, shards(): tile_sums.reshape(-1, emb_width).at[anchor_ids]  26.7 us
    dot_general x8, matrix products, score_block(): jnp.dot(pick, table_flat, preferred_element_type=jnp.float32)  23.2 us
  transfers between devices with their start and end apart: 6, of which 6 were waited for; matrix products, arithmetic and copies ran while one was open for 3% of the time, Pallas kernels for 0%

commit v1 on v0

v1 whole, which is shorter than its diff:
```python
import functools

import jax
import jax.numpy as jnp
from jax import lax
from jax.experimental import pallas as pl
from jax.experimental.pallas import tpu as pltpu
from jax.sharding import PartitionSpec as P

TILE = 128
ABLK = 128

SCORE_SCALE = 8.0
EPSILON = 1e-06
VMEM_LIMIT = 60 * 1024 * 1024
CHUNK = 256

ONE_COPY = pl.Buffered(1)


def whole(shape):
    return pl.BlockSpec(shape, lambda *_: (0,) * len(shape), pipeline_mode=ONE_COPY)


def node_forward(feature_rows, w_in, b_in, w_out):
    pre_act = jnp.dot(feature_rows, w_in, preferred_element_type=jnp.float32) + b_in
    hidden = jax.nn.silu(pre_act).astype(jnp.bfloat16)
    embedding = jnp.dot(hidden, w_out, preferred_element_type=jnp.float32)
    spread = jnp.sqrt(jnp.mean(embedding * embedding, axis=1, keepdims=True) + EPSILON)
    unit_rows = (embedding / spread).astype(jnp.bfloat16)
    return (pre_act, hidden, embedding, spread, unit_rows)


def rows_of(index, count=TILE):
    return pl.ds(pl.multiple_of(index * count, count), count)


def pick_kernel(asked_ref, table_ref, out_ref):
    def step(slot, carry):
        out_ref[rows_of(slot), :] = table_ref[rows_of(asked_ref[slot]), :]
        return carry

    lax.fori_loop(0, out_ref.shape[0] // TILE, step, 0, unroll=2)


def pick_tiles(asked, table, slots):
    shape = (slots * TILE, table.shape[1])
    return pl.pallas_call(
        pick_kernel,
        out_shape=jax.ShapeDtypeStruct(shape, table.dtype),
        grid_spec=pltpu.PrefetchScalarGridSpec(
            num_scalar_prefetch=1,
            grid=(1,),
            in_specs=[whole(table.shape)],
            out_specs=whole(shape),
        ),
        compiler_params=pltpu.CompilerParams(vmem_limit_bytes=VMEM_LIMIT),
    )(asked, table)


def score_kernel(
    local_count,
    remote_count,
    slot_count,
    lanes,
    ids_ref,
    tiles_ref,
    refs_ref,
    counts_ref,
    table_ref,
    fetched_ref,
    teacher_ref,
    kl_ref,
    local_grad_ref,
    remote_grad_ref,
    table_f,
    remote_acc,
    context,
    delta,
    anchor_rows,
    anchor_grad,
    *row_accs,
):
    block = pl.program_id(0)
    width = table_ref.shape[1]
    scale = SCORE_SCALE / width
    zero_chunk = jnp.zeros((CHUNK, width), jnp.float32)

    @pl.when(block == 0)
    def _():
        def clear(index, carry):
            here = rows_of(index, CHUNK)
            table_f[here, :] = table_ref[here, :].astype(jnp.float32)
            local_grad_ref[here, :] = zero_chunk
            for acc in row_accs:
                acc[here, :] = zero_chunk
            return carry

        lax.fori_loop(0, table_f.shape[0] // CHUNK, clear, 0)

        def clear_remote(index, carry):
            remote_acc[rows_of(index, CHUNK), :] = zero_chunk
            return carry

        lax.fori_loop(0, remote_acc.shape[0] // CHUNK, clear_remote, 0)

    rows = [ids_ref[block * ABLK + row] for row in range(ABLK)]
    for row in range(ABLK):
        anchor_rows[row : row + 1, :] = table_f[pl.ds(rows[row], 1), :]
    anchors = (anchor_rows[...] * scale).astype(jnp.bfloat16)

    places = []
    lives = []
    for i in range(local_count):
        place = rows_of(tiles_ref[block * local_count + i])
        context[i * TILE : (i + 1) * TILE, :] = table_ref[place, :]
        places.append(place)
        lives.append(None)
    for i in range(remote_count):
        ref = refs_ref[block * remote_count + i]
        place = rows_of(ref)
        at = local_count + i
        context[at * TILE : (at + 1) * TILE, :] = fetched_ref[place, :]
        places.append(place)
        live = lax.rem(ref, slot_count) < counts_ref[lax.div(ref, slot_count)]
        lives.append(jnp.where(live, 1.0, 0.0).astype(jnp.float32))

    student = []
    target = []
    student_sum = target_sum = gap_sum = None
    for i in range(local_count + remote_count):
        span = slice(i * TILE, (i + 1) * TILE)
        scores = lax.dot_general(
            anchors,
            context[span, :],
            (((1,), (1,)), ((), ())),
            preferred_element_type=jnp.float32,
        )
        teacher = teacher_ref[:, span].astype(jnp.float32)
        student_exp = jnp.exp(scores)
        target_exp = jnp.exp(teacher)
        if lives[i] is not None:
            student_exp = student_exp * lives[i]
            target_exp = target_exp * lives[i]
        gap = target_exp * (teacher - scores)
        student_sum = student_exp if i == 0 else student_sum + student_exp
        target_sum = target_exp if i == 0 else target_sum + target_exp
        gap_sum = gap if i == 0 else gap_sum + gap
        student.append(student_exp)
        target.append(target_exp)
    student_total = jnp.sum(student_sum, axis=1, keepdims=True)
    target_total = jnp.sum(target_sum, axis=1, keepdims=True)
    gap_total = jnp.sum(gap_sum, axis=1, keepdims=True)
    student_inv = 1.0 / student_total
    target_inv = 1.0 / target_total
    divergence = gap_total * target_inv - jnp.log(target_total) + jnp.log(student_total)
    kl_ref[0] = jnp.broadcast_to(divergence, (ABLK, TILE)).T[0:1, :]
    for i in range(local_count + remote_count):
        span = slice(i * TILE, (i + 1) * TILE)
        delta[:, span] = (student[i] * student_inv - target[i] * target_inv).astype(jnp.bfloat16)
    anchor_grad[...] = (
        jnp.dot(delta[...], context[...], preferred_element_type=jnp.float32) * scale
    )
    for i in range(local_count + remote_count):
        span = slice(i * TILE, (i + 1) * TILE)
        context_grad = lax.dot_general(
            delta[:, span],
            anchors,
            (((0,), (0,)), ((), ())),
            preferred_element_type=jnp.float32,
        )
        acc = local_grad_ref if i < local_count else remote_acc
        acc[places[i], :] += context_grad
    for row in range(ABLK):
        acc = row_accs[row % lanes]
        acc[pl.ds(rows[row], 1), :] += anchor_grad[row : row + 1, :]

    @pl.when(block == pl.num_programs(0) - 1)
    def _():
        def finish(index, carry):
            here = rows_of(index, CHUNK)
            total = local_grad_ref[here, :]
            for acc in row_accs:
                total = total + acc[here, :]
            local_grad_ref[here, :] = total
            return carry

        lax.fori_loop(0, table_f.shape[0] // CHUNK, finish, 0)

        def finish_remote(index, carry):
            here = rows_of(index, CHUNK)
            remote_grad_ref[here, :] = remote_acc[here, :].astype(jnp.bfloat16)
            return carry

        lax.fori_loop(0, remote_acc.shape[0] // CHUNK, finish_remote, 0)


def score(anchor_ids, local_tiles, remote_refs, own_counts, table, fetched, teacher, slot_count):
    blocks, local_count = local_tiles.shape
    remote_count = remote_refs.shape[1]
    context_width = teacher.shape[1]
    width = table.shape[1]
    lanes = 4 if table.shape[0] <= 8192 else 1
    kernel = functools.partial(score_kernel, local_count, remote_count, slot_count, lanes)
    kl, local_grad, remote_grad = pl.pallas_call(
        kernel,
        out_shape=(
            jax.ShapeDtypeStruct((blocks, 1, ABLK), jnp.float32),
            jax.ShapeDtypeStruct(table.shape, jnp.float32),
            jax.ShapeDtypeStruct(fetched.shape, jnp.bfloat16),
        ),
        grid_spec=pltpu.PrefetchScalarGridSpec(
            num_scalar_prefetch=4,
            grid=(blocks,),
            in_specs=[
                whole(table.shape),
                whole(fetched.shape),
                pl.BlockSpec((ABLK, context_width), lambda b, *_: (b, 0)),
            ],
            out_specs=(
                pl.BlockSpec((1, 1, ABLK), lambda b, *_: (b, 0, 0)),
                whole(table.shape),
                whole(fetched.shape),
            ),
            scratch_shapes=[
                pltpu.VMEM(table.shape, jnp.float32),
                pltpu.VMEM(fetched.shape, jnp.float32),
                pltpu.VMEM((context_width, width), jnp.bfloat16),
                pltpu.VMEM((ABLK, context_width), jnp.bfloat16),
                pltpu.VMEM((ABLK, width), jnp.float32),
                pltpu.VMEM((ABLK, width), jnp.float32),
            ]
            + [pltpu.VMEM(table.shape, jnp.float32)] * lanes,
        ),
        compiler_params=pltpu.CompilerParams(vmem_limit_bytes=VMEM_LIMIT),
    )(
        anchor_ids,
        local_tiles.reshape(-1),
        remote_refs.reshape(-1),
        own_counts,
        table,
        fetched,
        teacher,
    )
    return kl.reshape(-1), local_grad, remote_grad


def merge_kernel(asked_ref, local_ref, returned_ref, out_ref, acc):
    def load(index, carry):
        here = rows_of(index, CHUNK)
        acc[here, :] = local_ref[here, :]
        return carry

    lax.fori_loop(0, acc.shape[0] // CHUNK, load, 0)

    def add(slot, carry):
        acc[rows_of(asked_ref[slot]), :] += returned_ref[rows_of(slot), :].astype(jnp.float32)
        return carry

    lax.fori_loop(0, returned_ref.shape[0] // TILE, add, 0)

    def store(index, carry):
        here = rows_of(index, CHUNK)
        out_ref[here, :] = acc[here, :].astype(jnp.bfloat16)
        return carry

    lax.fori_loop(0, acc.shape[0] // CHUNK, store, 0)


def merge(asked, local_grad, returned):
    return pl.pallas_call(
        merge_kernel,
        out_shape=jax.ShapeDtypeStruct(local_grad.shape, jnp.bfloat16),
        grid_spec=pltpu.PrefetchScalarGridSpec(
            num_scalar_prefetch=1,
            grid=(1,),
            in_specs=[whole(local_grad.shape), whole(returned.shape)],
            out_specs=whole(local_grad.shape),
            scratch_shapes=[pltpu.VMEM(local_grad.shape, jnp.float32)],
        ),
        compiler_params=pltpu.CompilerParams(vmem_limit_bytes=VMEM_LIMIT),
    )(asked, local_grad, returned)


def shards(
    features, w_in, b_in, w_out, anchor_ids, local_tiles, requests, counts, remote_refs, teacher
):
    groups = lax.axis_size("group")
    devices = groups * lax.axis_size("dom")
    own_requests = requests[0, 0]
    own_counts = counts[0, 0]
    slot_count = own_requests.shape[1]
    every_request = lax.all_gather(own_requests, "group", axis=0, tiled=False)
    asked = lax.dynamic_index_in_dim(
        every_request, lax.axis_index("group"), axis=1, keepdims=False
    ).reshape(-1)
    pre_act, hidden, embedding, spread, unit_rows = node_forward(features, w_in, b_in, w_out)
    table = lax.all_gather(unit_rows, "dom", axis=0, tiled=True)
    served = pick_tiles(asked, table, groups * slot_count)
    fetched = lax.all_to_all(served, "group", split_axis=0, concat_axis=0, tiled=True)
    anchor_kl, local_grad, remote_grad = score(
        anchor_ids, local_tiles, remote_refs, own_counts, table, fetched, teacher, slot_count
    )
    returned = lax.all_to_all(remote_grad, "group", split_axis=0, concat_axis=0, tiled=True)
    merged = merge(asked, local_grad, returned)
    node_grad = lax.psum_scatter(merged, "dom", scatter_dimension=0, tiled=True).astype(
        jnp.float32
    )
    normed = embedding / spread
    embed_grad = (
        (node_grad - normed * jnp.mean(node_grad * normed, axis=1, keepdims=True)) / spread
    ).astype(jnp.bfloat16)
    out_grad = jnp.dot(hidden.T, embed_grad, preferred_element_type=jnp.float32)
    hidden_grad = jnp.dot(embed_grad, w_out.T, preferred_element_type=jnp.float32)
    sigmoid_pre = jax.nn.sigmoid(pre_act)
    pre_grad = hidden_grad * sigmoid_pre * (1.0 + pre_act * (1.0 - sigmoid_pre))
    bias_grad = jnp.sum(pre_grad, axis=0)
    in_grad_t = jnp.dot(
        pre_grad.astype(jnp.bfloat16).T, features, preferred_element_type=jnp.float32
    )
    hid = in_grad_t.shape[0]
    width = out_grad.shape[1]
    bias_rows = bias_grad.reshape(-1, width)
    used = 2 * hid + bias_rows.shape[0]
    unit = devices * 16
    padding = -used % unit
    stacked = jnp.concatenate(
        [in_grad_t, out_grad, bias_rows, jnp.zeros((padding, width), jnp.float32)], axis=0
    )
    part = lax.psum_scatter(stacked, "dom", scatter_dimension=0, tiled=True)
    part = lax.psum_scatter(part, "group", scatter_dimension=0, tiled=True)
    part = part * (1.0 / devices)
    part = lax.all_gather(part, "group", axis=0, tiled=True)
    totals = lax.all_gather(part, "dom", axis=0, tiled=True)
    return (
        anchor_kl,
        node_grad,
        totals[:hid].T,
        totals[2 * hid : used].reshape(-1),
        totals[hid : 2 * hid],
    )


def solution(mesh):
    return jax.shard_map(
        shards,
        mesh=mesh,
        in_specs=(
            P(("group", "dom"), None),
            P(),
            P(),
            P(),
            P(("group", "dom")),
            P(("group", "dom"), None),
            P("group", "dom", None, None),
            P("group", "dom", None),
            P(("group", "dom"), None),
            P(("group", "dom"), None),
        ),
        out_specs=(P(("group", "dom")), P(("group", "dom"), None), P(), P(), P()),
        check_vma=False,
    )
```

time: 656 us -> 397 us (0.61)
  local copies, waits for them, and re-layouts: 134 us -> 9.74 us
  other arithmetic: 98 us -> 6.01 us
  matrix products: 90 us -> 15.8 us
  waiting for transfers between devices: 255 us -> 190 us
  blocking collectives: 50.6 us -> 104 us
  Pallas kernels: 0 us -> 49.8 us
    psum x1 -> x0, waiting for transfers between devices: 88.5 us -> none  [shards(): totals = lax.psum((in_grad, bias_grad, out_grad), ('group', 'dom'))]
    dot_general x35 -> x1, matrix products: 74.8 us -> 1.29 us  [shards(): jnp.dot(pre_grad.astype(jnp.bfloat16).T, features, preferred_element_type...]
    reduce_scatter x2 -> x3, waiting for transfers between devices: 67.5 us -> 122 us  [the longest x1 62.5 us: shards(): part = lax.psum_scatter(part, 'group', scatter_dimension=0, tiled=True)]
    all_gather x0 -> x2, blocking collectives: none -> 51.7 us  [the longest x1 26.5 us: shards(): part = lax.all_gather(part, 'group', axis=0, tiled=True)]
    pallas_call x0 -> x3, Pallas kernels: none -> 49.8 us  [the longest x1 39.6 us: score(): pl.pallas_call(kernel, out_shape=(jax.ShapeDtypeStruct((blocks, 1, ABLK),...]
    all_to_all x2 -> x1, waiting for transfers between devices: 85.2 us -> 42.6 us  [shards(): lax.all_to_all(served, 'group', split_axis=0, concat_axis=0, tiled=True)]
    all_to_all x1, blocking collectives: 11.5 us -> 52.6 us  [shards(): lax.all_to_all(remote_grad, 'group', split_axis=0, concat_axis=0, tiled=T...]
    gather x25 -> x0, local copies, waits for them, and re-layouts: 40.3 us -> none  [the longest x8 30.2 us: score_block(): anchor_vecs = table_rows[anchor_block]]
  transfers between devices with their start and end apart: 6 -> 6, of which waited for: 6 -> 5; matrix products, arithmetic and copies ran while one was open for 3% -> 1% of each run, Pallas kernels for 0% -> 0%
where the time goes in v1:
time: 397 us; the launch traced here: 395 us
  waiting for transfers between devices  190 us (48%)
  blocking collectives  104 us (26%)
  Pallas kernels  49.8 us (13%)
  matrix products  15.8 us (4%)
  between operations  13.9 us (4%)
  local copies, waits for them, and re-layouts  9.74 us (2%)
  other arithmetic  6.01 us (2%)
  starting transfers between devices  5.39 us (1%)
    reduce_scatter x1, waiting for transfers between devices, shards(): part = lax.psum_scatter(part, 'group', scatter_dimension=0, tiled=True)  62.5 us
    all_to_all x1, blocking collectives, shards(): lax.all_to_all(remote_grad, 'group', split_axis=0, concat_axis=0, tiled=T...  52.6 us
    all_to_all x1, waiting for transfers between devices, shards(): lax.all_to_all(served, 'group', split_axis=0, concat_axis=0, tiled=True)  42.6 us
    pallas_call x1, Pallas kernels, score(): pl.pallas_call(kernel, out_shape=(jax.ShapeDtypeStruct((blocks, 1, ABLK),...  39.6 us
    reduce_scatter x1, waiting for transfers between devices, shards(): lax.psum_scatter(merged, 'dom', scatter_dimension=0, tiled=True)  32.6 us
    reduce_scatter x1, waiting for transfers between devices, shards(): part = lax.psum_scatter(stacked, 'dom', scatter_dimension=0, tiled=True)  26.6 us
    all_gather x1, blocking collectives, shards(): part = lax.all_gather(part, 'group', axis=0, tiled=True)  26.5 us
    all_gather x1, waiting for transfers between devices, shards(): totals = lax.all_gather(part, 'dom', axis=0, tiled=True)  26 us
  transfers between devices with their start and end apart: 6, of which 5 were waited for; matrix products, arithmetic and copies ran while one was open for 1% of the time, Pallas kernels for 0%

profile of v1, /device:TPU:1, one launch (start us, length us, event | category | flops | bytes accessed | tf_op | source)
XLA Modules:
  0.0 395.5 jit_solution(3086566300225803296)
XLA Ops:
  7.2 0.0 copy-start
  7.2 0.0 copy-start.4
  7.2 0.0 all-gather.4.cloned.1.call-start
  7.2 1.0 copy-done
  8.2 5.3 %multiply_convert_fusion = (bf16[2048,1024]{1,0:T(8,128)(2,1)S(1)}, f32[2048,1024]{1,0:T(8,128)}) fusion(f32[1024]{0:T(1024)} %param.12, bf16[2048,128]{1,0:T(8,128)(2,1)S(1)} %copy-done, bf16[128,1024]{1,0:T(8,128)(2,1)} %param.11), kind=kOutput, calls=%fused_computation.1 | convolution fusion | flops 549453824 | bytes 13373440 | tf_op jit(solution)/shard_map/dot_general | solution.py:26
  13.6 2.0 copy-done.1
  15.5 1.5 multiply_reduce_fusion.1
  17.1 0.3 copy.25
  17.4 1.1 fusion.2
  18.5 0.0 all-gather.4.cloned.1.call-update
  18.6 25.2 %all-gather = s32[8,1,8,8]{3,2,1,0:T(8,128)S(1)} all-gather(s32[1,1,8,8]{3,2,1,0:T(8,128)S(1)} %copy-done.5), channel_id=2, replica_groups=mesh['group'=8,'dom'=4] {'group'}, dimensions={0}, use_global_device_ids=true | all-gather | bytes 2304 | tf_op jit(solution)/shard_map/all_gather | solution.py:293
  43.8 0.6 reshape.48.asked_ref
  44.4 4.0 %shard_map.137 = bf16[8192,128]{1,0:T(8,128)(2,1)} custom-call(s32[64]{0:T(128)} %reshape.48.asked_ref, bf16[8192,128]{1,0:T(8,128)(2,1)} %all-gather.4.cloned.1.call-done.table_ref), custom_call_target="tpu_custom_call" | custom-call | tf_op jit(solution)/shard_map/pallas_call | solution.py:48
  48.4 5.2 %all-to-all-start = ((bf16[8,1024,128]{2,1,0:T(8,128)(2,1)}), bf16[8,1024,128]{2,1,0:T(8,128)(2,1)}, u32[]{:S(2)}, u32[]{:S(2)}) async-start(bf16[8,1024,128]{2,1,0:T(8,128)(2,1)} %bitcast.21), calls=%async_computation | async-start | bytes 4194304 | tf_op jit(solution)/shard_map/all_to_all | solution.py:300
  53.6 0.0 reduce-scatter.4.cloned.1.call-start
  53.7 0.1 copy.23
  53.8 0.6 reshape.46.tiles_ref
  54.4 0.1 copy.24
  54.5 0.6 reshape.47.refs_ref
  55.1 42.6 %all-to-all-done = bf16[8,1024,128]{2,1,0:T(8,128)(2,1)} async-done(((bf16[8,1024,128]{2,1,0:T(8,128)(2,1)}), bf16[8,1024,128]{2,1,0:T(8,128)(2,1)}, u32[]{:S(2)}, u32[]{:S(2)}) %all-to-all-start) | async-done | bytes 2097184 | tf_op jit(solution)/shard_map/all_to_all | solution.py:300
  97.7 39.6 %shard_map.138 = (f32[32,1,128]{2,1,0:T(1,128)}, f32[8192,128]{1,0:T(8,128)}, bf16[8192,128]{1,0:T(8,128)(2,1)}) custom-call(s32[4096]{0:T(1024)} %ids_ref.1, s32[128]{0:T(128)} %reshape.46.tiles_ref, s32[128]{0:T(128)} %reshape.47.refs_ref, s32[8]{0:T(128)} %bitcast.25, bf16[8192,128]{1,0:T(8,128)(2,1)} %all-gather.4.cloned.1.call-done.table_ref, ...), custom_call_target="tpu_custom_call" | custom-call | tf_op jit(solution)/shard_map/pallas_call | solution.py:205
  137.3 52.6 %all_to_all.22 = bf16[8,1024,128]{2,1,0:T(8,128)(2,1)} all-to-all(bf16[8,1024,128]{2,1,0:T(8,128)(2,1)} %bitcast.23), channel_id=1, replica_groups=mesh['group'=8,'dom'=4] {'group'}, dimensions={0} | all-to-all | bytes 4194304 | tf_op jit(solution)/shard_map/all_to_all | solution.py:304
  189.9 6.2 %shard_map.139 = bf16[8192,128]{1,0:T(8,128)(2,1)} custom-call(s32[64]{0:T(128)} %reshape.48.asked_ref, f32[8192,128]{1,0:T(8,128)} %get-tuple-element.9.local_ref, bf16[8192,128]{1,0:T(8,128)(2,1)} %bitcast.22), custom_call_target="tpu_custom_call" | custom-call | tf_op jit(solution)/shard_map/pallas_call | solution.py:271
  196.1 0.0 reduce-scatter.4.cloned.1.call-update
  196.1 0.0 reduce-scatter.6.cloned.1.call-start
  196.2 0.1 pad.3.clone
  196.2 32.6 %reduce-scatter.4.cloned.1.call-done = bf16[2048,128]{1,0:T(8,128)(2,1)} async-done(((bf16[8192,128]{1,0:T(8,128)(2,1)}), bf16[2048,128]{1,0:T(8,128)(2,1)}) %reduce-scatter.4.cloned.1.call-update) | async-done | bytes 524304 | tf_op jit(solution)/shard_map/reduce_scatter | solution.py:306
  228.9 1.8 multiply_reduce_fusion
  230.7 0.0 copy-start.3
  230.8 0.0 copy-start.8
  230.8 0.7 divide_convert_fusion
  231.5 1.3 fusion.5
  232.8 6.4 %fusion.4 = (f32[1024]{0:T(1024)S(1)}, bf16[2048,1024]{1,0:T(8,128)(2,1)S(1)}) fusion(f32[2048,1024]{1,0:T(8,128)} %get-tuple-element.31, f32[1024]{0:T(1024)S(1)} %copy-done.8, bf16[2048,128]{1,0:T(8,128)(2,1)S(1)} %divide_convert_fusion, bf16[1024,128]{1,0:T(8,128)(2,1)S(1)} %copy-done.4), kind=kOutput, calls=%fused_computation.18 | convolution fusion | flops 559938560 | bytes 13377536 | tf_op jit(solution)/shard_map/dot_general | solution.py:314
  239.2 1.3 fusion
  240.5 1.5 maximum_maximum_fusion
  242.0 0.0 reduce-scatter.6.cloned.1.call-update
  242.0 0.0 reduce-scatter.8.cloned.1.call-start
  242.1 26.6 %reduce-scatter.6.cloned.1.call-done = f32[640,128]{1,0:T(8,128)} async-done(((f32[2560,128]{1,0:T(8,128)}), f32[640,128]{1,0:T(8,128)}) %reduce-scatter.6.cloned.1.call-update) | async-done | bytes 327696 | tf_op jit(solution)/shard_map/reduce_scatter | solution.py:330
  268.7 0.0 reduce-scatter.8.cloned.1.call-update
  268.8 0.0 all-gather.6.cloned.1.call-start
  268.8 62.5 %reduce-scatter.8.cloned.1.call-done = f32[80,128]{1,0:T(8,128)} async-done(((f32[640,128]{1,0:T(8,128)}), f32[80,128]{1,0:T(8,128)}) %reduce-scatter.8.cloned.1.call-update) | async-done | bytes 40976 | tf_op jit(solution)/shard_map/reduce_scatter | solution.py:331
  331.3 0.8 broadcast_multiply_fusion
  332.1 26.5 %all_gather.14 = f32[640,128]{1,0:T(8,128)} all-gather(f32[80,128]{1,0:T(8,128)S(1)} %broadcast_multiply_fusion), channel_id=1, replica_groups=mesh['group'=8,'dom'=4] {'group'}, dimensions={0}, use_global_device_ids=true | all-gather | bytes 368640 | tf_op jit(solution)/shard_map/all_gather | solution.py:333
  358.6 0.0 all-gather.6.cloned.1.call-update
  358.6 26.0 %all-gather.6.cloned.1.call-done = f32[2560,128]{1,0:T(8,128)} async-done(((f32[640,128]{1,0:T(8,128)}), f32[2560,128]{1,0:T(8,128)}) %all-gather.6.cloned.1.call-update) | async-done | bytes 1310736 | tf_op jit(solution)/shard_map/all_gather | solution.py:334
  384.6 2.1 fusion.3
  386.6 1.0 copy.26
  387.6 1.3 slice_bitcast_fusion.1
  (17 shorter events, 0.1 us)
Async XLA Ops:
  7.2 1.0 copy-start
  7.2 8.3 %copy-start.4 = (bf16[1024,128]{1,0:T(8,128)(2,1)S(1)}, bf16[1024,128]{1,0:T(8,128)(2,1)}, u32[]{:S(2)}) copy-start(bf16[1024,128]{1,0:T(8,128)(2,1)} %param.13) | copy-start | bytes 786436
  7.2 37.2 %all-gather.4.cloned.1.call-start = ((), (), s32[]{:S(2)}) async-start(), calls=%async_computation.5 | async-start | bytes 2621440 | tf_op jit(solution)/shard_map/all_gather | solution.py:298
  13.6 2.0 copy-start.1
  15.5 3.1 copy-start.5
  44.4 9.3 %copy-start.6 = (s32[32,4]{0,1:T(4,128)S(1)}, s32[32,4]{0,1:T(4,128)}, u32[]{:S(2)}) copy-start(s32[32,4]{0,1:T(4,128)} %param.15) | copy-start | bytes 1540
  44.4 10.0 %copy-start.7 = (s32[32,4]{0,1:T(4,128)S(1)}, s32[32,4]{0,1:T(4,128)}, u32[]{:S(2)}) copy-start(s32[32,4]{0,1:T(4,128)} %param.18) | copy-start | bytes 1540
  48.4 49.2 %all-to-all-start = ((bf16[8,1024,128]{2,1,0:T(8,128)(2,1)}), bf16[8,1024,128]{2,1,0:T(8,128)(2,1)}, u32[]{:S(2)}, u32[]{:S(2)}) async-start(bf16[8,1024,128]{2,1,0:T(8,128)(2,1)} %bitcast.21), calls=%async_computation | async-start | bytes 4194304 | tf_op jit(solution)/shard_map/all_to_all | solution.py:300
  53.6 175.3 %reduce-scatter.4.cloned.1.call-start = ((), (), s32[]{:S(2)}) async-start(), calls=%async_computation.6 | async-start | bytes 2621440 | tf_op jit(solution)/shard_map/reduce_scatter | solution.py:306
  196.1 72.6 %reduce-scatter.6.cloned.1.call-start = ((), (), s32[]{:S(2)}) async-start(), calls=%async_computation.7 | async-start | bytes 1638400 | tf_op jit(solution)/shard_map/reduce_scatter | solution.py:330
  228.9 2.6 copy-start.2
  230.7 2.1 copy-start.3
  230.8 2.1 copy-start.8
  242.0 89.2 %reduce-scatter.8.cloned.1.call-start = ((), (), s32[]{:S(2)}) async-start(), calls=%async_computation.8 | async-start | bytes 368640 | tf_op jit(solution)/shard_map/reduce_scatter | solution.py:331
  268.8 115.8 %all-gather.6.cloned.1.call-start = ((), (), s32[]{:S(2)}) async-start(), calls=%async_computation.9 | async-start | bytes 1638400 | tf_op jit(solution)/shard_map/all_gather | solution.py:334
Sparse Core Ops, SparseCore 0:
  18.7 25.0 all-gather.3
  196.2 32.6 reduce-scatter.3
  242.2 26.5 reduce-scatter.5
  271.9 59.3 reduce-scatter.7
  358.7 25.7 all-gather.5

commit v2 on v1

--- a/solution.py
+++ b/solution.py
@@ -282,20 +282,255 @@
     )(asked, local_grad, returned)
 
 
+MESH = pl.DeviceIdType.MESH
+ANYWHERE = pl.BlockSpec(memory_space=pl.ANY)
+IN_VMEM = pl.BlockSpec(memory_space=pltpu.VMEM)
+
+
+def greet(partners):
+    barrier = pltpu.get_barrier_semaphore()
+    for partner in partners:
+        pl.semaphore_signal(barrier, inc=1, device_id=partner, device_id_type=MESH)
+    pl.semaphore_wait(barrier, len(partners))
+
+
+def push(src, dst, sems, index, partner):
+    copy = pltpu.make_async_remote_copy(
+        src_ref=src,
+        dst_ref=dst,
+        send_sem=sems[0].at[index],
+        recv_sem=sems[1].at[index],
+        device_id=partner,
+        device_id_type=MESH,
+    )
+    copy.start()
+    return copy
+
+
+def dom_partners(doms):
+    group, dom = lax.axis_index("group"), lax.axis_index("dom")
+    chips = doms // 2
+    chip, core = dom // 2, dom % 2
+    other = chip * 2 + (1 - core)
+    ahead = [lax.rem(chip + k, chips) * 2 + core for k in range(1, chips)]
+    behind = [lax.rem(chip + chips - k, chips) for k in range(1, chips)]
+    return group, dom, core, other, ahead, behind
+
+
+def gather_kernel(
+    groups, doms, unit_ref, requests_ref, table_ref, asked_ref,
+    own_sem, near_send, near_recv, far_send, far_recv, on_send, on_recv, ask_send, ask_recv,
+):
+    group, dom, core, other, ahead, behind = dom_partners(doms)
+    count = unit_ref.shape[0]
+    peers = [lax.rem(group + k, groups) for k in range(1, groups)]
+    greet([(group, other)] + [(group, far) for far in ahead] + [(peer, dom) for peer in peers])
+    here = table_ref.at[rows_of(dom, count), :]
+    far_copies = [
+        push(unit_ref, here, (far_send, far_recv), k, (group, far)) for k, far in enumerate(ahead)
+    ]
+    ask_copies = [
+        push(requests_ref.at[peer], asked_ref.at[group], (ask_send, ask_recv), k, (peer, dom))
+        for k, peer in enumerate(peers)
+    ]
+    near = push(unit_ref, here, (near_send, near_recv), 0, (group, other))
+    own = pltpu.make_async_copy(unit_ref, here, own_sem.at[0])
+    own.start()
+    own_ask = pltpu.make_async_copy(requests_ref.at[group], asked_ref.at[group], own_sem.at[1])
+    own_ask.start()
+    on_copies = []
+    for k, copy in enumerate(far_copies):
+        copy.wait_recv()
+        block = table_ref.at[rows_of(behind[k] * 2 + core, count), :]
+        on_copies.append(push(block, block, (on_send, on_recv), k, (group, other)))
+    own.wait()
+    own_ask.wait()
+    near.wait()
+    for copy in ask_copies:
+        copy.wait()
+    for copy in far_copies:
+        copy.wait_send()
+    for copy in on_copies:
+        copy.wait()
+
+
+def gather_table(unit_rows, own_requests, groups, doms):
+    slots = own_requests.shape[1]
+    asks = jnp.broadcast_to(own_requests[:, None, :], (groups, 8, slots))
+    asks = jnp.pad(asks, ((0, 0), (0, 0), (0, 128 - slots)))
+    far, peers = max(doms // 2 - 1, 1), max(groups - 1, 1)
+    dma = pltpu.SemaphoreType.DMA
+    table, asked = pl.pallas_call(
+        functools.partial(gather_kernel, groups, doms),
+        out_shape=(
+            jax.ShapeDtypeStruct((doms * unit_rows.shape[0], unit_rows.shape[1]), unit_rows.dtype),
+            jax.ShapeDtypeStruct(asks.shape, asks.dtype),
+        ),
+        in_specs=[ANYWHERE, ANYWHERE],
+        out_specs=(ANYWHERE, ANYWHERE),
+        scratch_shapes=[
+            dma((2,)), dma((1,)), dma((1,)), dma((far,)), dma((far,)),
+            dma((far,)), dma((far,)), dma((peers,)), dma((peers,)),
+        ],
+        compiler_params=pltpu.CompilerParams(collective_id=0, has_side_effects=True),
+    )(unit_rows, asks)
+    return table, asked[:, 0, :slots].reshape(-1)
+
+
+def scatter_kernel(
+    doms, merged_ref, out_ref, mine, kept, near_got, far_out, far_got,
+    own_sem, near_send, near_recv, far_send, far_recv,
+):
+    group, dom, core, other, ahead, behind = dom_partners(doms)
+    count = out_ref.shape[0]
+    chips = doms // 2
+    greet([(group, other)] + [(group, far) for far in ahead])
+    order = [dom // 2] + [lax.rem(dom // 2 + k, chips) for k in range(1, chips)]
+    order = order[1:] + order[:1]
+    near_copies = []
+    own_copies = []
+    for k, chip in enumerate(order):
+        theirs = merged_ref.at[rows_of(chip * 2 + (1 - core), count), :]
+        near_copies.append(push(theirs, near_got.at[k], (near_send, near_recv), k, (group, other)))
+        ours = merged_ref.at[rows_of(chip * 2 + core, count), :]
+        copy = pltpu.make_async_copy(ours, mine.at[k], own_sem.at[k])
+        copy.start()
+        own_copies.append(copy)
+    far_copies = []
+    for k in range(chips - 1):
+        near_copies[k].wait_recv()
+        own_copies[k].wait()
+        total = mine[k].astype(jnp.float32) + near_got[k].astype(jnp.float32)
+        far_out[k] = total.astype(jnp.bfloat16)
+        far_copies.append(
+            push(far_out.at[k], far_got.at[k], (far_send, far_recv), k, (group, ahead[k]))
+        )
+    near_copies[chips - 1].wait_recv()
+    own_copies[chips - 1].wait()
+    kept[...] = mine[chips - 1].astype(jnp.float32) + near_got[chips - 1].astype(jnp.float32)
+    for k, copy in enumerate(far_copies):
+        copy.wait_recv()
+        kept[...] += far_got[k].astype(jnp.float32)
+    out_ref[...] = kept[...]
+    for copy in near_copies + far_copies:
+        copy.wait_send()
+
+
+def scatter_sums(merged, doms):
+    count, width = merged.shape[0] // doms, merged.shape[1]
+    chips = doms // 2
+    far = max(chips - 1, 1)
+    dma = pltpu.SemaphoreType.DMA
+    return pl.pallas_call(
+        functools.partial(scatter_kernel, doms),
+        out_shape=jax.ShapeDtypeStruct((count, width), jnp.float32),
+        in_specs=[ANYWHERE],
+        out_specs=IN_VMEM,
+        scratch_shapes=[
+            pltpu.VMEM((chips, count, width), jnp.bfloat16),
+            pltpu.VMEM((count, width), jnp.float32),
+            pltpu.VMEM((chips, count, width), jnp.bfloat16),
+            pltpu.VMEM((far, count, width), jnp.bfloat16),
+            pltpu.VMEM((far, count, width), jnp.bfloat16),
+            dma((chips,)), dma((chips,)), dma((chips,)), dma((far,)), dma((far,)),
+        ],
+        compiler_params=pltpu.CompilerParams(
+            collective_id=1, has_side_effects=True, vmem_limit_bytes=VMEM_LIMIT
+        ),
+    )(merged)
+
+
+def totals_kernel(
+    groups, doms, x_ref, out_ref, out1, got1, part, out2, got2, gather1, gather2,
+    send1, recv1, send2, recv2, send3, recv3, send4, recv4,
+):
+    group, dom = lax.axis_index("group"), lax.axis_index("dom")
+    wide = x_ref.shape[0] // doms
+    thin = wide // groups
+    dom_peers = [lax.rem(dom + k, doms) for k in range(1, doms)]
+    group_peers = [lax.rem(group + k, groups) for k in range(1, groups)]
+    greet([(group, peer) for peer in dom_peers] + [(peer, dom) for peer in group_peers])
+    copies = []
+    first = []
+    for k, peer in enumerate(dom_peers):
+        out1[k] = x_ref[rows_of(peer, wide), :].astype(jnp.bfloat16)
+        first.append(push(out1.at[k], got1.at[k], (send1, recv1), k, (group, peer)))
+    part[...] = x_ref[rows_of(dom, wide), :]
+    for k, copy in enumerate(first):
+        copy.wait_recv()
+        part[...] += got1[k].astype(jnp.float32)
+    copies += first
+    second = []
+    for k, peer in enumerate(group_peers):
+        out2[k] = part[rows_of(peer, thin), :].astype(jnp.bfloat16)
+        second.append(push(out2.at[k], got2.at[k], (send2, recv2), k, (peer, dom)))
+    total = part[rows_of(group, thin), :]
+    for k, copy in enumerate(second):
+        copy.wait_recv()
+        total = total + got2[k].astype(jnp.float32)
+    copies += second
+    gather1[group] = (total * (1.0 / (groups * doms))).astype(jnp.bfloat16)
+    mine = gather1.at[group]
+    third = [
+        push(mine, mine, (send3, recv3), k, (peer, dom)) for k, peer in enumerate(group_peers)
+    ]
+    for copy in third:
+        copy.wait_recv()
+    copies += third
+    fourth = [
+        push(gather1, gather2.at[dom], (send4, recv4), k, (group, peer))
+        for k, peer in enumerate(dom_peers)
+    ]
+    out_ref[dom] = gather1[...].astype(jnp.float32)
+    for k, copy in enumerate(fourth):
+        copy.wait_recv()
+        source = lax.rem(dom + doms - (k + 1), doms)
+        out_ref[source] = gather2[source].astype(jnp.float32)
+    copies += fourth
+    for copy in copies:
+        copy.wait_send()
+
+
+def mean_over_devices(x, groups, doms):
+    rows, width = x.shape
+    wide = rows // doms
+    thin = wide // groups
+    a, b = max(doms - 1, 1), max(groups - 1, 1)
+    half = jnp.bfloat16
+    dma = pltpu.SemaphoreType.DMA
+    out = pl.pallas_call(
+        functools.partial(totals_kernel, groups, doms),
+        out_shape=jax.ShapeDtypeStruct((doms, groups, thin, width), jnp.float32),
+        in_specs=[IN_VMEM],
+        out_specs=IN_VMEM,
+        scratch_shapes=[
+            pltpu.VMEM((a, wide, width), half),
+            pltpu.VMEM((a, wide, width), half),
+            pltpu.VMEM((wide, width), jnp.float32),
+            pltpu.VMEM((b, thin, width), half),
+            pltpu.VMEM((b, thin, width), half),
+            pltpu.VMEM((groups, thin, width), half),
+            pltpu.VMEM((doms, groups, thin, width), half),
+            dma((a,)), dma((a,)), dma((b,)), dma((b,)), dma((b,)), dma((b,)), dma((a,)), dma((a,)),
+        ],
+        compiler_params=pltpu.CompilerParams(
+            collective_id=2, has_side_effects=True, vmem_limit_bytes=VMEM_LIMIT
+        ),
+    )(x)
+    return out.reshape(rows, width)
+
+
 def shards(
     features, w_in, b_in, w_out, anchor_ids, local_tiles, requests, counts, remote_refs, teacher
 ):
     groups = lax.axis_size("group")
-    devices = groups * lax.axis_size("dom")
+    doms = lax.axis_size("dom")
+    devices = groups * doms
     own_requests = requests[0, 0]
     own_counts = counts[0, 0]
     slot_count = own_requests.shape[1]
-    every_request = lax.all_gather(own_requests, "group", axis=0, tiled=False)
-    asked = lax.dynamic_index_in_dim(
-        every_request, lax.axis_index("group"), axis=1, keepdims=False
-    ).reshape(-1)
     pre_act, hidden, embedding, spread, unit_rows = node_forward(features, w_in, b_in, w_out)
-    table = lax.all_gather(unit_rows, "dom", axis=0, tiled=True)
+    table, asked = gather_table(unit_rows, own_requests, groups, doms)
     served = pick_tiles(asked, table, groups * slot_count)
     fetched = lax.all_to_all(served, "group", split_axis=0, concat_axis=0, tiled=True)
     anchor_kl, local_grad, remote_grad = score(
@@ -303,9 +538,7 @@
     )
     returned = lax.all_to_all(remote_grad, "group", split_axis=0, concat_axis=0, tiled=True)
     merged = merge(asked, local_grad, returned)
-    node_grad = lax.psum_scatter(merged, "dom", scatter_dimension=0, tiled=True).astype(
-        jnp.float32
-    )
+    node_grad = scatter_sums(merged, doms)
     normed = embedding / spread
     embed_grad = (
         (node_grad - normed * jnp.mean(node_grad * normed, axis=1, keepdims=True)) / spread
@@ -327,11 +560,7 @@
     stacked = jnp.concatenate(
         [in_grad_t, out_grad, bias_rows, jnp.zeros((padding, width), jnp.float32)], axis=0
     )
-    part = lax.psum_scatter(stacked, "dom", scatter_dimension=0, tiled=True)
-    part = lax.psum_scatter(part, "group", scatter_dimension=0, tiled=True)
-    part = part * (1.0 / devices)
-    part = lax.all_gather(part, "group", axis=0, tiled=True)
-    totals = lax.all_gather(part, "dom", axis=0, tiled=True)
+    totals = mean_over_devices(stacked, groups, doms)
     return (
         anchor_kl,
         node_grad,

time: 397 us -> 260 us (0.65)
  blocking collectives: 104 us -> 0 us
  waiting for transfers between devices: 190 us -> 93 us
  Pallas kernels: 49.8 us -> 122 us
  between operations: 13.9 us -> 0.8 us
    reduce_scatter x3 -> x0, waiting for transfers between devices: 122 us -> none  [the longest x1 62.5 us: shards(): part = lax.psum_scatter(part, 'group', scatter_dimension=0, tiled=True)]
    pallas_call x0 -> x3, Pallas kernels: none -> 71.9 us  [the longest x1 30.2 us: mean_over_devices(): pl.pallas_call(functools.partial(totals_kernel, groups, doms), out_shape=...]
    all_to_all x1 -> x0, blocking collectives: 52.6 us -> none  [shards(): lax.all_to_all(remote_grad, 'group', split_axis=0, concat_axis=0, tiled=T...]
    all_gather x2 -> x0, blocking collectives: 51.7 us -> none  [the longest x1 26.5 us: shards(): part = lax.all_gather(part, 'group', axis=0, tiled=True)]
    all_to_all x0 -> x1, waiting for transfers between devices: none -> 47 us  [shards(): lax.all_to_all(remote_grad, 'group', split_axis=0, concat_axis=0, tiled=T...]
    all_gather x2 -> x0, waiting for transfers between devices: 26 us -> none  [the longest x1 26 us: shards(): totals = lax.all_gather(part, 'dom', axis=0, tiled=True)]
    all_to_all x0 -> x1, starting transfers between devices: none -> 4.64 us  [shards(): lax.all_to_all(remote_grad, 'group', split_axis=0, concat_axis=0, tiled=T...]
  transfers between devices with their start and end apart: 6 -> 2, of which waited for: 5 -> 2; matrix products, arithmetic and copies ran while one was open for 1% -> 1% of each run, Pallas kernels for 0% -> 0%
where the time goes in v2:
time: 260 us; the launch traced here: 259 us
  Pallas kernels  122 us (47%)
  waiting for transfers between devices  93 us (36%)
  matrix products  15.8 us (6%)
  local copies, waits for them, and re-layouts  12.1 us (5%)
  starting transfers between devices  8.98 us (3%)
  other arithmetic  6.4 us (2%)
    all_to_all x1, waiting for transfers between devices, shards(): lax.all_to_all(remote_grad, 'group', split_axis=0, concat_axis=0, tiled=T...  47 us
    all_to_all x1, waiting for transfers between devices, shards(): lax.all_to_all(served, 'group', split_axis=0, concat_axis=0, tiled=True)  45.9 us
    pallas_call x1, Pallas kernels, score(): pl.pallas_call(kernel, out_shape=(jax.ShapeDtypeStruct((blocks, 1, ABLK),...  39.6 us
    pallas_call x1, Pallas kernels, mean_over_devices(): pl.pallas_call(functools.partial(totals_kernel, groups, doms), out_shape=...  30.2 us
    pallas_call x1, Pallas kernels, gather_table(): pl.pallas_call(functools.partial(gather_kernel, groups, doms), out_shape=...  22.4 us
    pallas_call x1, Pallas kernels, scatter_sums(): pl.pallas_call(functools.partial(scatter_kernel, doms), out_shape=jax.Sha...  19.2 us
    dot_general x1, matrix products, shards(): jnp.dot(embed_grad, w_out.T, preferred_element_type=jnp.float32)  6.34 us
    pallas_call x1, Pallas kernels, merge(): pl.pallas_call(merge_kernel, out_shape=jax.ShapeDtypeStruct(local_grad.sh...  6.19 us
  transfers between devices with their start and end apart: 2, of which 2 were waited for; matrix products, arithmetic and copies ran while one was open for 1% of the time, Pallas kernels for 0%

profile of v2, /device:TPU:1, one launch (start us, length us, event | category | flops | bytes accessed | tf_op | source)
XLA Modules:
  0.0 258.8 jit_solution(13640731398597045032)
XLA Ops:
  0.6 0.0 copy-start
  0.6 0.0 copy-start.4
  0.7 1.0 copy-done
  1.7 5.4 %multiply_convert_fusion = (bf16[2048,1024]{1,0:T(8,128)(2,1)S(1)}, f32[2048,1024]{1,0:T(8,128)}) fusion(f32[1024]{0:T(1024)} %param.12, bf16[2048,128]{1,0:T(8,128)(2,1)S(1)} %copy-done, bf16[128,1024]{1,0:T(8,128)(2,1)} %param.11), kind=kOutput, calls=%fused_computation.1 | convolution fusion | flops 549453824 | bytes 13373440 | tf_op jit(solution)/shard_map/dot_general | solution.py:26
  7.0 0.0 copy-start.1
  7.0 2.0 copy-done.1
  9.0 0.0 copy-done.4
  9.0 0.0 copy-start.5
  9.0 1.5 multiply_reduce_fusion.1
  10.6 0.3 copy.21
  10.9 1.1 fusion.2.unit_ref
  12.0 0.0 copy-done.5
  12.0 0.6 pad.4.requests_ref
  12.7 22.4 %shard_map.137 = (bf16[8192,128]{1,0:T(8,128)(2,1)}, s32[8,8,128]{2,1,0:T(8,128)}) custom-call(bf16[2048,128]{1,0:T(8,128)(2,1)} %fusion.2.unit_ref, s32[8,8,128]{2,1,0:T(8,128)} %pad.4.requests_ref), custom_call_target="tpu_custom_call" | custom-call | tf_op jit(solution)/shard_map/pallas_call | solution.py:363
  35.1 0.8 slice_reduce_fusion
  35.9 0.6 reshape_squeeze.3.asked_ref
  36.5 4.0 %shard_map.138 = bf16[8192,128]{1,0:T(8,128)(2,1)} custom-call(s32[64]{0:T(128)} %reshape_squeeze.3.asked_ref, bf16[8192,128]{1,0:T(8,128)(2,1)} %get-tuple-element.10.table_ref), custom_call_target="tpu_custom_call" | custom-call | tf_op jit(solution)/shard_map/pallas_call | solution.py:48
  40.5 4.3 %all-to-all-start = ((bf16[8,1024,128]{2,1,0:T(8,128)(2,1)}), bf16[8,1024,128]{2,1,0:T(8,128)(2,1)}, u32[]{:S(2)}, u32[]{:S(2)}) async-start(bf16[8,1024,128]{2,1,0:T(8,128)(2,1)} %bitcast.23), calls=%async_computation | async-start | bytes 4194304 | tf_op jit(solution)/shard_map/all_to_all | solution.py:535
  44.8 0.0 copy-done.6
  44.8 0.1 copy.19
  44.9 0.6 reshape.46.tiles_ref
  45.6 0.0 copy-done.7
  45.6 0.1 copy.20
  45.6 0.6 reshape.47.refs_ref
  46.3 45.9 %all-to-all-done = bf16[8,1024,128]{2,1,0:T(8,128)(2,1)} async-done(((bf16[8,1024,128]{2,1,0:T(8,128)(2,1)}), bf16[8,1024,128]{2,1,0:T(8,128)(2,1)}, u32[]{:S(2)}, u32[]{:S(2)}) %all-to-all-start) | async-done | bytes 2097184 | tf_op jit(solution)/shard_map/all_to_all | solution.py:535
  92.2 39.6 %shard_map.139 = (f32[32,1,128]{2,1,0:T(1,128)}, f32[8192,128]{1,0:T(8,128)}, bf16[8192,128]{1,0:T(8,128)(2,1)}) custom-call(s32[4096]{0:T(1024)} %ids_ref.1, s32[128]{0:T(128)} %reshape.46.tiles_ref, s32[128]{0:T(128)} %reshape.47.refs_ref, s32[8]{0:T(128)} %bitcast.29, bf16[8192,128]{1,0:T(8,128)(2,1)} %get-tuple-element.10.table_ref, ...), custom_call_target="tpu_custom_call" | custom-call | tf_op jit(solution)/shard_map/pallas_call | solution.py:205
  131.8 4.6 %all-to-all-start.1 = ((bf16[8,1024,128]{2,1,0:T(8,128)(2,1)}), bf16[8,1024,128]{2,1,0:T(8,128)(2,1)}, u32[]{:S(2)}, u32[]{:S(2)}) async-start(bf16[8,1024,128]{2,1,0:T(8,128)(2,1)} %bitcast.26), calls=%async_computation.1 | async-start | bytes 4194304 | tf_op jit(solution)/shard_map/all_to_all | solution.py:539
  136.5 0.1 pad.8.clone
  136.5 47.0 %all-to-all-done.1 = bf16[8,1024,128]{2,1,0:T(8,128)(2,1)} async-done(((bf16[8,1024,128]{2,1,0:T(8,128)(2,1)}), bf16[8,1024,128]{2,1,0:T(8,128)(2,1)}, u32[]{:S(2)}, u32[]{:S(2)}) %all-to-all-start.1) | async-done | bytes 2097184 | tf_op jit(solution)/shard_map/all_to_all | solution.py:539
  183.6 6.2 %shard_map.140.merged_ref = bf16[8192,128]{1,0:T(8,128)(2,1)} custom-call(s32[64]{0:T(128)} %reshape_squeeze.3.asked_ref, f32[8192,128]{1,0:T(8,128)} %get-tuple-element.13.local_ref, bf16[8192,128]{1,0:T(8,128)(2,1)} %bitcast.6.returned_ref), custom_call_target="tpu_custom_call" | custom-call | tf_op jit(solution)/shard_map/pallas_call | solution.py:271
  189.8 19.2 %shard_map.141 = f32[2048,128]{1,0:T(8,128)} custom-call(bf16[8192,128]{1,0:T(8,128)(2,1)} %shard_map.140.merged_ref), custom_call_target="tpu_custom_call" | custom-call | tf_op jit(solution)/shard_map/pallas_call | solution.py:424
  209.0 0.0 copy-start.2
  209.0 2.0 multiply_reduce_fusion
  211.0 0.0 copy-start.8
  211.1 1.8 divide_convert_fusion
  212.8 0.0 copy-done.2
  212.8 1.3 fusion.5
  214.1 0.0 copy-done.8
  214.1 6.3 %fusion.4 = (f32[1024]{0:T(1024)S(1)}, bf16[2048,1024]{1,0:T(8,128)(2,1)S(1)}) fusion(f32[2048,1024]{1,0:T(8,128)} %get-tuple-element.28, f32[1024]{0:T(1024)S(1)} %copy-done.8, bf16[2048,128]{1,0:T(8,128)(2,1)S(1)} %divide_convert_fusion, bf16[1024,128]{1,0:T(8,128)(2,1)S(1)} %copy-done.4), kind=kOutput, calls=%fused_computation.17 | convolution fusion | flops 559938560 | bytes 13377536 | tf_op jit(solution)/shard_map/dot_general | solution.py:547
  220.5 1.3 fusion
  221.8 0.0 copy-start.3
  221.8 1.5 maximum_maximum_fusion.x_ref
  223.3 30.2 %shard_map.142 = f32[4,8,80,128]{3,2,1,0:T(8,128)} custom-call(f32[2560,128]{1,0:T(8,128)} %maximum_maximum_fusion.x_ref), custom_call_target="tpu_custom_call" | custom-call | tf_op jit(solution)/shard_map/pallas_call | solution.py:501
  253.5 2.1 fusion.3
  255.6 1.3 slice_bitcast_fusion.1
  256.8 1.0 copy.22
  257.8 0.0 copy-done.3
  257.8 1.0 copy.24
  (6 shorter events, 0.0 us)
Async XLA Ops:
  0.6 1.0 copy-start
  0.6 8.4 %copy-start.4 = (bf16[1024,128]{1,0:T(8,128)(2,1)S(1)}, bf16[1024,128]{1,0:T(8,128)(2,1)}, u32[]{:S(2)}) copy-start(bf16[1024,128]{1,0:T(8,128)(2,1)} %param.13) | copy-start | bytes 786436
  7.0 2.0 copy-start.1
  9.0 3.0 %copy-start.5 = (s32[1,1,8,8]{3,2,1,0:T(8,128)S(1)}, s32[1,1,8,8]{3,2,1,0:T(8,128)}, u32[]{:S(2)}) copy-start(s32[1,1,8,8]{3,2,1,0:T(8,128)} %param.16) | copy-start | bytes 772
  36.5 8.4 %copy-start.6 = (s32[32,4]{0,1:T(4,128)S(1)}, s32[32,4]{0,1:T(4,128)}, u32[]{:S(2)}) copy-start(s32[32,4]{0,1:T(4,128)} %param.15) | copy-start | bytes 1540
  36.5 9.1 %copy-start.7 = (s32[32,4]{0,1:T(4,128)S(1)}, s32[32,4]{0,1:T(4,128)}, u32[]{:S(2)}) copy-start(s32[32,4]{0,1:T(4,128)} %param.18) | copy-start | bytes 1540
  40.5 51.7 %all-to-all-start = ((bf16[8,1024,128]{2,1,0:T(8,128)(2,1)}), bf16[8,1024,128]{2,1,0:T(8,128)(2,1)}, u32[]{:S(2)}, u32[]{:S(2)}) async-start(bf16[8,1024,128]{2,1,0:T(8,128)(2,1)} %bitcast.23), calls=%async_computation | async-start | bytes 4194304 | tf_op jit(solution)/shard_map/all_to_all | solution.py:535
  131.8 51.8 %all-to-all-start.1 = ((bf16[8,1024,128]{2,1,0:T(8,128)(2,1)}), bf16[8,1024,128]{2,1,0:T(8,128)(2,1)}, u32[]{:S(2)}, u32[]{:S(2)}) async-start(bf16[8,1024,128]{2,1,0:T(8,128)(2,1)} %bitcast.26), calls=%async_computation.1 | async-start | bytes 4194304 | tf_op jit(solution)/shard_map/all_to_all | solution.py:539
  209.0 3.8 %copy-start.2 = (bf16[2048,1024]{1,0:T(8,128)(2,1)S(1)}, bf16[2048,1024]{1,0:T(8,128)(2,1)}, u32[]{:S(2)}) copy-start(bf16[2048,1024]{1,0:T(8,128)(2,1)} %copy-done.1) | copy-start | bytes 12582916
  211.0 3.1 %copy-start.8 = (f32[1024]{0:T(1024)S(1)}, f32[1024]{0:T(1024)}, u32[]{:S(2)}) copy-start(f32[1024]{0:T(1024)} %param.12) | copy-start | bytes 12292
  221.8 36.0 %copy-start.3 = (f32[2048,128]{1,0:T(8,128)S(1)}, f32[2048,128]{1,0:T(8,128)}, u32[]{:S(2)}) copy-start(f32[2048,128]{1,0:T(8,128)} %shard_map.141) | copy-start | bytes 3145732

commit v3 on v2

--- a/solution.py
+++ b/solution.py
@@ -1,4 +1,5 @@
 import functools
+import math
 
 import jax
 import jax.numpy as jnp
@@ -58,124 +59,264 @@
     )(asked, table)
 
 
-def score_kernel(
-    local_count,
-    remote_count,
-    slot_count,
-    lanes,
-    ids_ref,
-    tiles_ref,
-    refs_ref,
-    counts_ref,
-    table_ref,
-    fetched_ref,
-    teacher_ref,
-    kl_ref,
-    local_grad_ref,
-    remote_grad_ref,
-    table_f,
-    remote_acc,
-    context,
-    delta,
-    anchor_rows,
-    anchor_grad,
-    *row_accs,
+def cost(flops, moved, powers):
+    return pl.CostEstimate(flops=flops, bytes_accessed=moved, transcendentals=powers)
+
+
+def clear_rows(ref):
+    zero_chunk = jnp.zeros((CHUNK, ref.shape[1]), ref.dtype)
+
+    def clear(index, carry):
+        ref[rows_of(index, CHUNK), :] = zero_chunk
+        return carry
+
+    lax.fori_loop(0, ref.shape[0] // CHUNK, clear, 0)
+
+
+def as_row(column):
+    return jnp.broadcast_to(column, (ABLK, TILE)).T[0:1, :]
+
+
+def prepare_kernel(
+    per_step, local_count, remote_count, slot_count, ids_ref, refs_ref, counts_ref,
+    table_ref, teacher_ref, anchors_ref, target_ref, base_ref, table_f, anchor_rows,
 ):
-    block = pl.program_id(0)
-    width = table_ref.shape[1]
-    scale = SCORE_SCALE / width
-    zero_chunk = jnp.zeros((CHUNK, width), jnp.float32)
-
-    @pl.when(block == 0)
+    scale = SCORE_SCALE / table_ref.shape[1]
+
+    @pl.when(pl.program_id(0) == 0)
     def _():
-        def clear(index, carry):
+        def widen(index, carry):
             here = rows_of(index, CHUNK)
             table_f[here, :] = table_ref[here, :].astype(jnp.float32)
-            local_grad_ref[here, :] = zero_chunk
-            for acc in row_accs:
-                acc[here, :] = zero_chunk
             return carry
 
-        lax.fori_loop(0, table_f.shape[0] // CHUNK, clear, 0)
-
-        def clear_remote(index, carry):
-            remote_acc[rows_of(index, CHUNK), :] = zero_chunk
-            return carry
-
-        lax.fori_loop(0, remote_acc.shape[0] // CHUNK, clear_remote, 0)
-
-    rows = [ids_ref[block * ABLK + row] for row in range(ABLK)]
-    for row in range(ABLK):
-        anchor_rows[row : row + 1, :] = table_f[pl.ds(rows[row], 1), :]
-    anchors = (anchor_rows[...] * scale).astype(jnp.bfloat16)
-
+        lax.fori_loop(0, table_f.shape[0] // CHUNK, widen, 0)
+
+    for sub in range(per_step):
+        block = pl.program_id(0) * per_step + sub
+        rows = slice(sub * ABLK, (sub + 1) * ABLK)
+        for row in range(ABLK):
+            at = sub * ABLK + row
+            index = ids_ref[block * ABLK + row]
+            anchor_rows[at : at + 1, :] = table_f[pl.ds(index, 1), :]
+        target_sum = gap_sum = None
+        exps = []
+        for i in range(local_count + remote_count):
+            teacher = teacher_ref[rows, i * TILE : (i + 1) * TILE].astype(jnp.float32)
+            target_exp = jnp.exp(teacher)
+            if i >= local_count:
+                ref = refs_ref[block * remote_count + i - local_count]
+                live = lax.rem(ref, slot_count) < counts_ref[lax.div(ref, slot_count)]
+                target_exp = target_exp * jnp.where(live, 1.0, 0.0).astype(jnp.float32)
+            gap = target_exp * teacher
+            target_sum = target_exp if i == 0 else target_sum + target_exp
+            gap_sum = gap if i == 0 else gap_sum + gap
+            exps.append(target_exp)
+        total = jnp.sum(target_sum, axis=1, keepdims=True)
+        inverse = 1.0 / total
+        base = jnp.sum(gap_sum, axis=1, keepdims=True) * inverse - jnp.log(total)
+        base_ref[sub] = as_row(base)
+        for i, target_exp in enumerate(exps):
+            target_ref[rows, i * TILE : (i + 1) * TILE] = (target_exp * inverse).astype(
+                jnp.bfloat16
+            )
+    anchors_ref[...] = (anchor_rows[...] * scale).astype(jnp.bfloat16)
+
+
+def prepare(per_step, anchor_ids, remote_refs, local_count, own_counts, table, teacher, slots):
+    blocks, remote_count = remote_refs.shape
+    anchors, context_width = teacher.shape
+    width = table.shape[1]
+    rows = per_step * ABLK
+    return pl.pallas_call(
+        functools.partial(prepare_kernel, per_step, local_count, remote_count, slots),
+        out_shape=(
+            jax.ShapeDtypeStruct((anchors, width), jnp.bfloat16),
+            jax.ShapeDtypeStruct((anchors, context_width), jnp.bfloat16),
+            jax.ShapeDtypeStruct((blocks, 1, ABLK), jnp.float32),
+        ),
+        grid_spec=pltpu.PrefetchScalarGridSpec(
+            num_scalar_prefetch=3,
+            grid=(blocks // per_step,),
+            in_specs=[
+                whole(table.shape),
+                pl.BlockSpec((rows, context_width), lambda b, *_: (b, 0)),
+            ],
+            out_specs=(
+                pl.BlockSpec((rows, width), lambda b, *_: (b, 0)),
+                pl.BlockSpec((rows, context_width), lambda b, *_: (b, 0)),
+                pl.BlockSpec((per_step, 1, ABLK), lambda b, *_: (b, 0, 0)),
+            ),
+            scratch_shapes=[
+                pltpu.VMEM(table.shape, jnp.float32),
+                pltpu.VMEM((rows, width), jnp.float32),
+            ],
+        ),
+        compiler_params=pltpu.CompilerParams(vmem_limit_bytes=VMEM_LIMIT),
+        cost_estimate=cost(
+            10 * anchors * context_width, 4 * anchors * context_width, anchors * context_width
+        ),
+    )(anchor_ids, remote_refs.reshape(-1), own_counts, table, teacher)
+
+
+def take_context(block, sub, context, tiles_ref, refs_ref, table_ref, fetched_ref, counts):
+    local_count, remote_count = counts
     places = []
-    lives = []
     for i in range(local_count):
         place = rows_of(tiles_ref[block * local_count + i])
-        context[i * TILE : (i + 1) * TILE, :] = table_ref[place, :]
+        context[sub, i * TILE : (i + 1) * TILE, :] = table_ref[place, :]
         places.append(place)
-        lives.append(None)
     for i in range(remote_count):
-        ref = refs_ref[block * remote_count + i]
-        place = rows_of(ref)
+        place = rows_of(refs_ref[block * remote_count + i])
         at = local_count + i
-        context[at * TILE : (at + 1) * TILE, :] = fetched_ref[place, :]
+        context[sub, at * TILE : (at + 1) * TILE, :] = fetched_ref[place, :]
         places.append(place)
-        live = lax.rem(ref, slot_count) < counts_ref[lax.div(ref, slot_count)]
-        lives.append(jnp.where(live, 1.0, 0.0).astype(jnp.float32))
-
-    student = []
-    target = []
-    student_sum = target_sum = gap_sum = None
-    for i in range(local_count + remote_count):
-        span = slice(i * TILE, (i + 1) * TILE)
-        scores = lax.dot_general(
-            anchors,
-            context[span, :],
-            (((1,), (1,)), ((), ())),
-            preferred_element_type=jnp.float32,
+    return places
+
+
+def tile_grad(delta, anchors):
+    return lax.dot_general(
+        delta, anchors, (((0,), (0,)), ((), ())), preferred_element_type=jnp.float32
+    )
+
+
+def score_kernel(
+    per_step, local_count, remote_count, slot_count, tiles_ref, refs_ref, counts_ref,
+    table_ref, fetched_ref, anchors_ref, target_ref, base_ref,
+    kl_ref, delta_ref, remote_grad_ref, remote_acc, context,
+):
+    tiles = local_count + remote_count
+
+    @pl.when(pl.program_id(0) == 0)
+    def _():
+        clear_rows(remote_acc)
+
+    for sub in range(per_step):
+        block = pl.program_id(0) * per_step + sub
+        rows = slice(sub * ABLK, (sub + 1) * ABLK)
+        places = take_context(
+            block, sub, context, tiles_ref, refs_ref, table_ref, fetched_ref,
+            (local_count, remote_count),
         )
-        teacher = teacher_ref[:, span].astype(jnp.float32)
-        student_exp = jnp.exp(scores)
-        target_exp = jnp.exp(teacher)
-        if lives[i] is not None:
-            student_exp = student_exp * lives[i]
-            target_exp = target_exp * lives[i]
-        gap = target_exp * (teacher - scores)
-        student_sum = student_exp if i == 0 else student_sum + student_exp
-        target_sum = target_exp if i == 0 else target_sum + target_exp
-        gap_sum = gap if i == 0 else gap_sum + gap
-        student.append(student_exp)
-        target.append(target_exp)
-    student_total = jnp.sum(student_sum, axis=1, keepdims=True)
-    target_total = jnp.sum(target_sum, axis=1, keepdims=True)
-    gap_total = jnp.sum(gap_sum, axis=1, keepdims=True)
-    student_inv = 1.0 / student_total
-    target_inv = 1.0 / target_total
-    divergence = gap_total * target_inv - jnp.log(target_total) + jnp.log(student_total)
-    kl_ref[0] = jnp.broadcast_to(divergence, (ABLK, TILE)).T[0:1, :]
-    for i in range(local_count + remote_count):
-        span = slice(i * TILE, (i + 1) * TILE)
-        delta[:, span] = (student[i] * student_inv - target[i] * target_inv).astype(jnp.bfloat16)
-    anchor_grad[...] = (
-        jnp.dot(delta[...], context[...], preferred_element_type=jnp.float32) * scale
-    )
-    for i in range(local_count + remote_count):
-        span = slice(i * TILE, (i + 1) * TILE)
-        context_grad = lax.dot_general(
-            delta[:, span],
-            anchors,
-            (((0,), (0,)), ((), ())),
-            preferred_element_type=jnp.float32,
+        anchors = anchors_ref[rows, :]
+        student = []
+        student_sum = gap_sum = None
+        for i in range(tiles):
+            span = slice(i * TILE, (i + 1) * TILE)
+            scores = lax.dot_general(
+                anchors,
+                context[sub, span, :],
+                (((1,), (1,)), ((), ())),
+                preferred_element_type=jnp.float32,
+            )
+            student_exp = jnp.exp(scores)
+            if i >= local_count:
+                ref = refs_ref[block * remote_count + i - local_count]
+                live = lax.rem(ref, slot_count) < counts_ref[lax.div(ref, slot_count)]
+                student_exp = student_exp * jnp.where(live, 1.0, 0.0).astype(jnp.float32)
+            gap = target_ref[rows, span].astype(jnp.float32) * scores
+            student_sum = student_exp if i == 0 else student_sum + student_exp
+            gap_sum = gap if i == 0 else gap_sum + gap
+            student.append(student_exp)
+        total = jnp.sum(student_sum, axis=1, keepdims=True)
+        inverse = 1.0 / total
+        rest = jnp.log(total) - jnp.sum(gap_sum, axis=1, keepdims=True)
+        kl_ref[sub] = base_ref[sub] + as_row(rest)
+        for i in range(tiles):
+            span = slice(i * TILE, (i + 1) * TILE)
+            delta = (student[i] * inverse - target_ref[rows, span].astype(jnp.float32)).astype(
+                jnp.bfloat16
+            )
+            delta_ref[rows, span] = delta
+            if i >= local_count:
+                remote_acc[places[i], :] += tile_grad(delta, anchors)
+
+    @pl.when(pl.program_id(0) == pl.num_programs(0) - 1)
+    def _():
+        def finish(index, carry):
+            here = rows_of(index, CHUNK)
+            remote_grad_ref[here, :] = remote_acc[here, :].astype(jnp.bfloat16)
+            return carry
+
+        lax.fori_loop(0, remote_acc.shape[0] // CHUNK, finish, 0)
+
+
+def score(per_step, local_tiles, remote_refs, own_counts, table, fetched, prepared, slots):
+    anchors, target, base = prepared
+    blocks, local_count = local_tiles.shape
+    remote_count = remote_refs.shape[1]
+    context_width = target.shape[1]
+    width = table.shape[1]
+    rows = per_step * ABLK
+    pairs = target.shape[0] * context_width
+    return pl.pallas_call(
+        functools.partial(score_kernel, per_step, local_count, remote_count, slots),
+        out_shape=(
+            jax.ShapeDtypeStruct((blocks, 1, ABLK), jnp.float32),
+            jax.ShapeDtypeStruct(target.shape, jnp.bfloat16),
+            jax.ShapeDtypeStruct(fetched.shape, jnp.bfloat16),
+        ),
+        grid_spec=pltpu.PrefetchScalarGridSpec(
+            num_scalar_prefetch=3,
+            grid=(blocks // per_step,),
+            in_specs=[
+                whole(table.shape),
+                whole(fetched.shape),
+                pl.BlockSpec((rows, width), lambda b, *_: (b, 0)),
+                pl.BlockSpec((rows, context_width), lambda b, *_: (b, 0)),
+                pl.BlockSpec((per_step, 1, ABLK), lambda b, *_: (b, 0, 0)),
+            ],
+            out_specs=(
+                pl.BlockSpec((per_step, 1, ABLK), lambda b, *_: (b, 0, 0)),
+                pl.BlockSpec((rows, context_width), lambda b, *_: (b, 0)),
+                whole(fetched.shape),
+            ),
+            scratch_shapes=[
+                pltpu.VMEM(fetched.shape, jnp.float32),
+                pltpu.VMEM((per_step, context_width, width), jnp.bfloat16),
+            ],
+        ),
+        compiler_params=pltpu.CompilerParams(vmem_limit_bytes=VMEM_LIMIT),
+        cost_estimate=cost(3 * pairs * width, 4 * pairs, pairs),
+    )(
+        local_tiles.reshape(-1), remote_refs.reshape(-1), own_counts,
+        table, fetched, anchors, target, base,
+    )
+
+
+def local_kernel(
+    per_step, local_count, remote_count, lanes, ids_ref, tiles_ref, refs_ref,
+    table_ref, fetched_ref, anchors_ref, delta_ref, local_grad_ref,
+    context, anchor_grad, *row_accs,
+):
+    scale = SCORE_SCALE / table_ref.shape[1]
+
+    @pl.when(pl.program_id(0) == 0)
+    def _():
+        clear_rows(local_grad_ref)
+        for acc in row_accs:
+            clear_rows(acc)
+
+    for sub in range(per_step):
+        block = pl.program_id(0) * per_step + sub
+        rows = slice(sub * ABLK, (sub + 1) * ABLK)
+        places = take_context(
+            block, sub, context, tiles_ref, refs_ref, table_ref, fetched_ref,
+            (local_count, remote_count),
         )
-        acc = local_grad_ref if i < local_count else remote_acc
-        acc[places[i], :] += context_grad
-    for row in range(ABLK):
-        acc = row_accs[row % lanes]
-        acc[pl.ds(rows[row], 1), :] += anchor_grad[row : row + 1, :]
-
-    @pl.when(block == pl.num_programs(0) - 1)
+        anchor_grad[rows, :] = (
+            jnp.dot(delta_ref[rows, :], context[sub], preferred_element_type=jnp.float32) * scale
+        )
+        anchors = anchors_ref[rows, :]
+        for i in range(local_count):
+            span = slice(i * TILE, (i + 1) * TILE)
+            local_grad_ref[places[i], :] += tile_grad(delta_ref[rows, span], anchors)
+        for row in range(ABLK):
+            acc = row_accs[row % lanes]
+            at = sub * ABLK + row
+            acc[pl.ds(ids_ref[block * ABLK + row], 1), :] += anchor_grad[at : at + 1, :]
+
+    @pl.when(pl.program_id(0) == pl.num_programs(0) - 1)
     def _():
         def finish(index, carry):
             here = rows_of(index, CHUNK)
@@ -185,64 +326,42 @@
             local_grad_ref[here, :] = total
             return carry
 
-        lax.fori_loop(0, table_f.shape[0] // CHUNK, finish, 0)
-
-        def finish_remote(index, carry):
-            here = rows_of(index, CHUNK)
-            remote_grad_ref[here, :] = remote_acc[here, :].astype(jnp.bfloat16)
-            return carry
-
-        lax.fori_loop(0, remote_acc.shape[0] // CHUNK, finish_remote, 0)
-
-
-def score(anchor_ids, local_tiles, remote_refs, own_counts, table, fetched, teacher, slot_count):
+        lax.fori_loop(0, local_grad_ref.shape[0] // CHUNK, finish, 0)
+
+
+def local_grads(per_step, anchor_ids, local_tiles, remote_refs, table, fetched, anchors, delta):
     blocks, local_count = local_tiles.shape
     remote_count = remote_refs.shape[1]
-    context_width = teacher.shape[1]
+    context_width = delta.shape[1]
     width = table.shape[1]
+    rows = per_step * ABLK
     lanes = 4 if table.shape[0] <= 8192 else 1
-    kernel = functools.partial(score_kernel, local_count, remote_count, slot_count, lanes)
-    kl, local_grad, remote_grad = pl.pallas_call(
-        kernel,
-        out_shape=(
-            jax.ShapeDtypeStruct((blocks, 1, ABLK), jnp.float32),
-            jax.ShapeDtypeStruct(table.shape, jnp.float32),
-            jax.ShapeDtypeStruct(fetched.shape, jnp.bfloat16),
-        ),
+    pairs = delta.shape[0] * context_width
+    return pl.pallas_call(
+        functools.partial(local_kernel, per_step, local_count, remote_count, lanes),
+        out_shape=jax.ShapeDtypeStruct(table.shape, jnp.float32),
         grid_spec=pltpu.PrefetchScalarGridSpec(
-            num_scalar_prefetch=4,
-            grid=(blocks,),
+            num_scalar_prefetch=3,
+            grid=(blocks // per_step,),
             in_specs=[
                 whole(table.shape),
                 whole(fetched.shape),
-                pl.BlockSpec((ABLK, context_width), lambda b, *_: (b, 0)),
+                pl.BlockSpec((rows, width), lambda b, *_: (b, 0)),
+                pl.BlockSpec((rows, context_width), lambda b, *_: (b, 0)),
             ],
-            out_specs=(
-                pl.BlockSpec((1, 1, ABLK), lambda b, *_: (b, 0, 0)),
-                whole(table.shape),
-                whole(fetched.shape),
-            ),
+            out_specs=whole(table.shape),
             scratch_shapes=[
-                pltpu.VMEM(table.shape, jnp.float32),
-                pltpu.VMEM(fetched.shape, jnp.float32),
-                pltpu.VMEM((context_width, width), jnp.bfloat16),
-                pltpu.VMEM((ABLK, context_width), jnp.bfloat16),
-                pltpu.VMEM((ABLK, width), jnp.float32),
-                pltpu.VMEM((ABLK, width), jnp.float32),
+                pltpu.VMEM((per_step, context_width, width), jnp.bfloat16),
+                pltpu.VMEM((rows, width), jnp.float32),
             ]
             + [pltpu.VMEM(table.shape, jnp.float32)] * lanes,
         ),
         compiler_params=pltpu.CompilerParams(vmem_limit_bytes=VMEM_LIMIT),
+        cost_estimate=cost(3 * pairs * width, 2 * pairs, 0),
     )(
-        anchor_ids,
-        local_tiles.reshape(-1),
-        remote_refs.reshape(-1),
-        own_counts,
-        table,
-        fetched,
-        teacher,
-    )
-    return kl.reshape(-1), local_grad, remote_grad
+        anchor_ids, local_tiles.reshape(-1), remote_refs.reshape(-1),
+        table, fetched, anchors, delta,
+    )
 
 
 def merge_kernel(asked_ref, local_ref, returned_ref, out_ref, acc):
@@ -533,10 +652,19 @@
     table, asked = gather_table(unit_rows, own_requests, groups, doms)
     served = pick_tiles(asked, table, groups * slot_count)
     fetched = lax.all_to_all(served, "group", split_axis=0, concat_axis=0, tiled=True)
-    anchor_kl, local_grad, remote_grad = score(
-        anchor_ids, local_tiles, remote_refs, own_counts, table, fetched, teacher, slot_count
-    )
+    per_step = math.gcd(local_tiles.shape[0], 2)
+    prepared = prepare(
+        per_step, anchor_ids, remote_refs, local_tiles.shape[1], own_counts, table, teacher,
+        slot_count,
+    )
+    anchor_kl, delta, remote_grad = score(
+        per_step, local_tiles, remote_refs, own_counts, table, fetched, prepared, slot_count
+    )
+    anchor_kl = anchor_kl.reshape(-1)
     returned = lax.all_to_all(remote_grad, "group", split_axis=0, concat_axis=0, tiled=True)
+    local_grad = local_grads(
+        per_step, anchor_ids, local_tiles, remote_refs, table, fetched, prepared[0], delta
+    )
     merged = merge(asked, local_grad, returned)
     node_grad = scatter_sums(merged, doms)
     normed = embedding / spread

time: 260 us -> 248 us (0.954)
  waiting for transfers between devices: 93 us -> 55.7 us
  Pallas kernels: 122 us -> 144 us
  local copies, waits for them, and re-layouts: 12.1 us -> 14.8 us
    pallas_call x1 -> x3, Pallas kernels: 39.6 us -> 62.9 us  [the longest x1 25.2 us: score(): pl.pallas_call(functools.partial(score_kernel, per_step, local_count, rem...]
    all_to_all x1, waiting for transfers between devices: 47 us -> 26.6 us  [shards(): lax.all_to_all(remote_grad, 'group', split_axis=0, concat_axis=0, tiled=T...]
    all_to_all x1, waiting for transfers between devices: 45.9 us -> 29.1 us  [shards(): lax.all_to_all(served, 'group', split_axis=0, concat_axis=0, tiled=True)]
    unnamed x22 -> x30, local copies, waits for them, and re-layouts: 5.16 us -> 7.79 us
  transfers between devices with their start and end apart: 2 -> 2, of which waited for: 2 -> 2; matrix products, arithmetic and copies ran while one was open for 1% -> 1% of each run, Pallas kernels for 0% -> 15%
where the time goes in v3:
time: 248 us; the launch traced here: 246 us
  Pallas kernels  144 us (58%)
  waiting for transfers between devices  55.7 us (22%)
  matrix products  15.8 us (6%)
  local copies, waits for them, and re-layouts  14.8 us (6%)
  starting transfers between devices  8.27 us (3%)
  other arithmetic  6.41 us (3%)
    pallas_call x1, Pallas kernels, mean_over_devices(): pl.pallas_call(functools.partial(totals_kernel, groups, doms), out_shape=...  30.2 us
    all_to_all x1, waiting for transfers between devices, shards(): lax.all_to_all(served, 'group', split_axis=0, concat_axis=0, tiled=True)  29.1 us
    all_to_all x1, waiting for transfers between devices, shards(): lax.all_to_all(remote_grad, 'group', split_axis=0, concat_axis=0, tiled=T...  26.6 us
    pallas_call x1, Pallas kernels, score(): pl.pallas_call(functools.partial(score_kernel, per_step, local_count, rem...  25.2 us
    pallas_call x1, Pallas kernels, gather_table(): pl.pallas_call(functools.partial(gather_kernel, groups, doms), out_shape=...  22.4 us
    pallas_call x1, Pallas kernels, local_grads(): pl.pallas_call(functools.partial(local_kernel, per_step, local_count, rem...  20.9 us
    pallas_call x1, Pallas kernels, scatter_sums(): pl.pallas_call(functools.partial(scatter_kernel, doms), out_shape=jax.Sha...  18.5 us
    pallas_call x1, Pallas kernels, prepare(): pl.pallas_call(functools.partial(prepare_kernel, per_step, local_count, r...  16.8 us
  transfers between devices with their start and end apart: 2, of which 2 were waited for; matrix products, arithmetic and copies ran while one was open for 1% of the time, Pallas kernels for 15%

profile of v3, /device:TPU:1, one launch (start us, length us, event | category | flops | bytes accessed | tf_op | source)
XLA Modules:
  0.0 246.3 jit_solution(727920204746129803)
XLA Ops:
  0.6 0.0 copy-start
  0.6 0.0 copy-start.8
  0.7 1.0 copy-done
  1.7 5.3 %multiply_convert_fusion = (bf16[2048,1024]{1,0:T(8,128)(2,1)S(1)}, f32[2048,1024]{1,0:T(8,128)}) fusion(f32[1024]{0:T(1024)} %param.12, bf16[2048,128]{1,0:T(8,128)(2,1)S(1)} %copy-done, bf16[128,1024]{1,0:T(8,128)(2,1)} %param.11), kind=kOutput, calls=%fused_computation.1 | convolution fusion | flops 549453824 | bytes 13373440 | tf_op jit(solution)/shard_map/dot_general | solution.py:27
  7.0 2.0 copy-done.1
  9.0 0.0 copy-done.8
  9.0 1.5 multiply_reduce_fusion.1
  10.5 0.3 copy.21
  10.8 0.0 copy-start.5
  10.9 1.1 fusion.2.unit_ref
  12.0 0.0 copy-done.9
  12.0 0.6 pad.4.requests_ref
  12.6 22.4 %shard_map.137 = (bf16[8192,128]{1,0:T(8,128)(2,1)}, s32[8,8,128]{2,1,0:T(8,128)}) custom-call(bf16[2048,128]{1,0:T(8,128)(2,1)} %fusion.2.unit_ref, s32[8,8,128]{2,1,0:T(8,128)} %pad.4.requests_ref), custom_call_target="tpu_custom_call" | custom-call | tf_op jit(solution)/shard_map/pallas_call | solution.py:482
  35.1 0.8 slice_reduce_fusion
  35.8 0.6 reshape_squeeze.3.asked_ref
  36.4 4.1 %shard_map.138 = bf16[8192,128]{1,0:T(8,128)(2,1)} custom-call(s32[64]{0:T(128)} %reshape_squeeze.3.asked_ref, bf16[8192,128]{1,0:T(8,128)(2,1)} %get-tuple-element.13.table_ref), custom_call_target="tpu_custom_call" | custom-call | tf_op jit(solution)/shard_map/pallas_call | solution.py:49
  40.5 0.0 copy-done.5
  40.5 3.6 %all-to-all-start = ((bf16[8,1024,128]{2,1,0:T(8,128)(2,1)}), bf16[8,1024,128]{2,1,0:T(8,128)(2,1)S(1)}, u32[]{:S(2)}, u32[]{:S(2)}) async-start(bf16[8,1024,128]{2,1,0:T(8,128)(2,1)} %bitcast.25), calls=%async_computation | async-start | bytes 4194304 | tf_op jit(solution)/shard_map/all_to_all | solution.py:654
  44.1 0.0 copy-done.10
  44.1 0.1 copy.20
  44.2 0.6 reshape.50.refs_ref
  44.8 0.0 copy-done.11
  44.8 0.1 copy.19
  44.9 0.6 reshape.49.tiles_ref
  45.5 16.8 %shard_map.139 = (bf16[4096,128]{1,0:T(8,128)(2,1)}, bf16[4096,1024]{1,0:T(8,128)(2,1)}, f32[32,1,128]{2,1,0:T(1,128)}) custom-call(s32[4096]{0:T(1024)} %ids_ref.3, s32[128]{0:T(128)} %reshape.50.refs_ref, s32[8]{0:T(128)} %bitcast.32, bf16[8192,128]{1,0:T(8,128)(2,1)} %get-tuple-element.13.table_ref, bf16[4096,1024]{1,0:T(8,128)(2,1)} %teacher_ref.1), custom_call_target="tpu_custom_call" | custom-call | flops 41943040 | bytes 16777216 | tf_op jit(solution)/shard_map/pallas_call | solution.py:131
  62.3 29.1 %all-to-all-done = bf16[8,1024,128]{2,1,0:T(8,128)(2,1)S(1)} async-done(((bf16[8,1024,128]{2,1,0:T(8,128)(2,1)}), bf16[8,1024,128]{2,1,0:T(8,128)(2,1)S(1)}, u32[]{:S(2)}, u32[]{:S(2)}) %all-to-all-start) | async-done | bytes 2097184 | tf_op jit(solution)/shard_map/all_to_all | solution.py:654
  91.4 1.3 copy-done.3
  92.7 25.2 %shard_map.140 = (f32[32,1,128]{2,1,0:T(1,128)}, bf16[4096,1024]{1,0:T(8,128)(2,1)}, bf16[8192,128]{1,0:T(8,128)(2,1)}) custom-call(s32[128]{0:T(128)} %reshape.49.tiles_ref, s32[128]{0:T(128)} %reshape.50.refs_ref, s32[8]{0:T(128)} %bitcast.33, bf16[8192,128]{1,0:T(8,128)(2,1)} %get-tuple-element.13.table_ref, bf16[8192,128]{1,0:T(8,128)(2,1)} %bitcast.23, ...), custom_call_target="tpu_custom_call" | custom-call | flops 1610612736 | bytes 16777216 | tf_op jit(solution)/shard_map/pallas_call | solution.py:252
  117.9 4.7 %all-to-all-start.1 = ((bf16[8,1024,128]{2,1,0:T(8,128)(2,1)}), bf16[8,1024,128]{2,1,0:T(8,128)(2,1)S(1)}, u32[]{:S(2)}, u32[]{:S(2)}) async-start(bf16[8,1024,128]{2,1,0:T(8,128)(2,1)} %bitcast.29), calls=%async_computation.1 | async-start | bytes 4194304 | tf_op jit(solution)/shard_map/all_to_all | solution.py:664
  122.6 0.1 pad.8.clone
  122.7 20.9 %shard_map.141.local_ref = f32[8192,128]{1,0:T(8,128)} custom-call(s32[4096]{0:T(1024)} %ids_ref.3, s32[128]{0:T(128)} %reshape.49.tiles_ref, s32[128]{0:T(128)} %reshape.50.refs_ref, bf16[8192,128]{1,0:T(8,128)(2,1)} %get-tuple-element.13.table_ref, bf16[8192,128]{1,0:T(8,128)(2,1)} %bitcast.24, bf16[4096,128]{1,0:T(8,128)(2,1)} %get-tuple-element.15.anchors_ref, ...), custom_call_target="tpu_custom_call" | custom-call | flops 1610612736 | bytes 8388608 | tf_op jit(solution)/shard_map/pallas_call | solution.py:340
  143.6 26.6 %all-to-all-done.1 = bf16[8,1024,128]{2,1,0:T(8,128)(2,1)S(1)} async-done(((bf16[8,1024,128]{2,1,0:T(8,128)(2,1)}), bf16[8,1024,128]{2,1,0:T(8,128)(2,1)S(1)}, u32[]{:S(2)}, u32[]{:S(2)}) %all-to-all-start.1) | async-done | bytes 2097184 | tf_op jit(solution)/shard_map/all_to_all | solution.py:664
  170.2 1.3 copy-done.7
  171.5 6.3 %shard_map.142.merged_ref = bf16[8192,128]{1,0:T(8,128)(2,1)} custom-call(s32[64]{0:T(128)} %reshape_squeeze.3.asked_ref, f32[8192,128]{1,0:T(8,128)} %shard_map.141.local_ref, bf16[8192,128]{1,0:T(8,128)(2,1)} %bitcast.26), custom_call_target="tpu_custom_call" | custom-call | tf_op jit(solution)/shard_map/pallas_call | solution.py:390
  177.9 18.5 %shard_map.143 = f32[2048,128]{1,0:T(8,128)} custom-call(bf16[8192,128]{1,0:T(8,128)(2,1)} %shard_map.142.merged_ref), custom_call_target="tpu_custom_call" | custom-call | tf_op jit(solution)/shard_map/pallas_call | solution.py:543
  196.4 2.0 multiply_reduce_fusion
  198.5 0.0 copy-start.12
  198.5 1.8 divide_convert_fusion
  200.2 0.0 copy-done.2
  200.3 1.3 fusion.5
  201.6 6.4 %fusion.4 = (f32[1024]{0:T(1024)S(1)}, bf16[2048,1024]{1,0:T(8,128)(2,1)S(1)}) fusion(f32[2048,1024]{1,0:T(8,128)} %get-tuple-element.34, f32[1024]{0:T(1024)S(1)} %copy-done.12, bf16[2048,128]{1,0:T(8,128)(2,1)S(1)} %divide_convert_fusion, bf16[1024,128]{1,0:T(8,128)(2,1)S(1)} %copy-done.8), kind=kOutput, calls=%fused_computation.17 | convolution fusion | flops 559938560 | bytes 13377536 | tf_op jit(solution)/shard_map/dot_general | solution.py:675
  207.9 1.3 fusion
  209.2 1.5 maximum_maximum_fusion.x_ref
  210.7 30.2 %shard_map.144 = f32[4,8,80,128]{3,2,1,0:T(8,128)} custom-call(f32[2560,128]{1,0:T(8,128)} %maximum_maximum_fusion.x_ref), custom_call_target="tpu_custom_call" | custom-call | tf_op jit(solution)/shard_map/pallas_call | solution.py:620
  241.0 2.1 fusion.3
  243.1 1.3 slice_bitcast_fusion.1
  244.3 1.0 copy.22
  245.3 1.0 copy.24
  (16 shorter events, 0.0 us)
Async XLA Ops:
  0.6 1.0 copy-start
  0.6 8.3 %copy-start.8 = (bf16[1024,128]{1,0:T(8,128)(2,1)S(1)}, bf16[1024,128]{1,0:T(8,128)(2,1)}, u32[]{:S(2)}) copy-start(bf16[1024,128]{1,0:T(8,128)(2,1)} %param.13) | copy-start | bytes 786436
  7.0 2.0 copy-start.1
  9.0 3.0 %copy-start.9 = (s32[1,1,8,8]{3,2,1,0:T(8,128)S(1)}, s32[1,1,8,8]{3,2,1,0:T(8,128)}, u32[]{:S(2)}) copy-start(s32[1,1,8,8]{3,2,1,0:T(8,128)} %param.16) | copy-start | bytes 772
  10.8 29.7 %copy-start.5 = (f32[2048,128]{1,0:T(8,128)}, f32[2048,128]{1,0:T(8,128)S(1)}, u32[]{:S(2)}) copy-start(f32[2048,128]{1,0:T(8,128)S(1)} %copy.21) | copy-start | bytes 3145732
  36.4 7.7 %copy-start.10 = (s32[32,4]{0,1:T(4,128)S(1)}, s32[32,4]{0,1:T(4,128)}, u32[]{:S(2)}) copy-start(s32[32,4]{0,1:T(4,128)} %param.18) | copy-start | bytes 1540
  36.4 8.4 %copy-start.11 = (s32[32,4]{0,1:T(4,128)S(1)}, s32[32,4]{0,1:T(4,128)}, u32[]{:S(2)}) copy-start(s32[32,4]{0,1:T(4,128)} %param.15) | copy-start | bytes 1540
  40.5 50.9 %all-to-all-start = ((bf16[8,1024,128]{2,1,0:T(8,128)(2,1)}), bf16[8,1024,128]{2,1,0:T(8,128)(2,1)S(1)}, u32[]{:S(2)}, u32[]{:S(2)}) async-start(bf16[8,1024,128]{2,1,0:T(8,128)(2,1)} %bitcast.25), calls=%async_computation | async-start | bytes 4194304 | tf_op jit(solution)/shard_map/all_to_all | solution.py:654
  91.4 1.3 copy-start.3
  117.9 52.3 %all-to-all-start.1 = ((bf16[8,1024,128]{2,1,0:T(8,128)(2,1)}), bf16[8,1024,128]{2,1,0:T(8,128)(2,1)S(1)}, u32[]{:S(2)}, u32[]{:S(2)}) async-start(bf16[8,1024,128]{2,1,0:T(8,128)(2,1)} %bitcast.29), calls=%async_computation.1 | async-start | bytes 4194304 | tf_op jit(solution)/shard_map/all_to_all | solution.py:664
  170.2 1.3 copy-start.7
  171.5 24.9 %copy-start.6 = (f32[2048,128]{1,0:T(8,128)S(1)}, f32[2048,128]{1,0:T(8,128)}, u32[]{:S(2)}) copy-start(f32[2048,128]{1,0:T(8,128)} %copy-done.5) | copy-start | bytes 3145732
  196.4 3.8 %copy-start.2 = (bf16[2048,1024]{1,0:T(8,128)(2,1)S(1)}, bf16[2048,1024]{1,0:T(8,128)(2,1)}, u32[]{:S(2)}) copy-start(bf16[2048,1024]{1,0:T(8,128)(2,1)} %copy-done.1) | copy-start | bytes 12582916
  198.5 3.1 %copy-start.12 = (f32[1024]{0:T(1024)S(1)}, f32[1024]{0:T(1024)}, u32[]{:S(2)}) copy-start(f32[1024]{0:T(1024)} %param.12) | copy-start | bytes 12292
  209.2 36.1 %copy-start.4 = (f32[2048,128]{1,0:T(8,128)S(1)}, f32[2048,128]{1,0:T(8,128)}, u32[]{:S(2)}) copy-start(f32[2048,128]{1,0:T(8,128)} %shard_map.143) | copy-start | bytes 3145732

commit v4 on v3

--- a/solution.py
+++ b/solution.py
@@ -77,9 +77,20 @@
     return jnp.broadcast_to(column, (ABLK, TILE)).T[0:1, :]
 
 
+def as_column(row):
+    return jnp.broadcast_to(row, (TILE, ABLK)).T[:, 0:1]
+
+
+def tile_scores(anchors, context):
+    return lax.dot_general(
+        anchors, context, (((1,), (1,)), ((), ())), preferred_element_type=jnp.float32
+    )
+
+
 def prepare_kernel(
-    per_step, local_count, remote_count, slot_count, ids_ref, refs_ref, counts_ref,
-    table_ref, teacher_ref, anchors_ref, target_ref, base_ref, table_f, anchor_rows,
+    per_step, local_count, remote_count, slot_count, ids_ref, tiles_ref, refs_ref, counts_ref,
+    table_ref, teacher_ref, anchors_ref, near_ref, far_ref, base_ref, partial_ref,
+    table_f, anchor_rows,
 ):
     scale = SCORE_SCALE / table_ref.shape[1]
 
@@ -99,7 +110,9 @@
             at = sub * ABLK + row
             index = ids_ref[block * ABLK + row]
             anchor_rows[at : at + 1, :] = table_f[pl.ds(index, 1), :]
-        target_sum = gap_sum = None
+        anchors = (anchor_rows[rows, :] * scale).astype(jnp.bfloat16)
+        anchors_ref[rows, :] = anchors
+        target_sum = gap_sum = student_sum = None
         exps = []
         for i in range(local_count + remote_count):
             teacher = teacher_ref[rows, i * TILE : (i + 1) * TILE].astype(jnp.float32)
@@ -108,7 +121,13 @@
                 ref = refs_ref[block * remote_count + i - local_count]
                 live = lax.rem(ref, slot_count) < counts_ref[lax.div(ref, slot_count)]
                 target_exp = target_exp * jnp.where(live, 1.0, 0.0).astype(jnp.float32)
-            gap = target_exp * teacher
+                gap = target_exp * teacher
+            else:
+                place = rows_of(tiles_ref[block * local_count + i])
+                scores = tile_scores(anchors, table_ref[place, :])
+                gap = target_exp * (teacher - scores)
+                student_exp = jnp.exp(scores)
+                student_sum = student_exp if i == 0 else student_sum + student_exp
             target_sum = target_exp if i == 0 else target_sum + target_exp
             gap_sum = gap if i == 0 else gap_sum + gap
             exps.append(target_exp)
@@ -116,15 +135,18 @@
         inverse = 1.0 / total
         base = jnp.sum(gap_sum, axis=1, keepdims=True) * inverse - jnp.log(total)
         base_ref[sub] = as_row(base)
+        partial_ref[sub] = as_row(jnp.sum(student_sum, axis=1, keepdims=True))
         for i, target_exp in enumerate(exps):
-            target_ref[rows, i * TILE : (i + 1) * TILE] = (target_exp * inverse).astype(
+            out_ref, at = (near_ref, i) if i < local_count else (far_ref, i - local_count)
+            out_ref[rows, at * TILE : (at + 1) * TILE] = (target_exp * inverse).astype(
                 jnp.bfloat16
             )
-    anchors_ref[...] = (anchor_rows[...] * scale).astype(jnp.bfloat16)
-
-
-def prepare(per_step, anchor_ids, remote_refs, local_count, own_counts, table, teacher, slots):
+
+
+def prepare(per_step, anchor_ids, local_tiles, remote_refs, own_counts, table, teacher, slots):
     blocks, remote_count = remote_refs.shape
+    local_count = local_tiles.shape[1]
+    near, far = local_count * TILE, remote_count * TILE
     anchors, context_width = teacher.shape
     width = table.shape[1]
     rows = per_step * ABLK
@@ -132,11 +154,13 @@
         functools.partial(prepare_kernel, per_step, local_count, remote_count, slots),
         out_shape=(
             jax.ShapeDtypeStruct((anchors, width), jnp.bfloat16),
-            jax.ShapeDtypeStruct((anchors, context_width), jnp.bfloat16),
+            jax.ShapeDtypeStruct((anchors, near), jnp.bfloat16),
+            jax.ShapeDtypeStruct((anchors, far), jnp.bfloat16),
             jax.ShapeDtypeStruct((blocks, 1, ABLK), jnp.float32),
+            jax.ShapeDtypeStruct((blocks, 1, ABLK), jnp.float32),
         ),
         grid_spec=pltpu.PrefetchScalarGridSpec(
-            num_scalar_prefetch=3,
+            num_scalar_prefetch=4,
             grid=(blocks // per_step,),
             in_specs=[
                 whole(table.shape),
@@ -144,7 +168,9 @@
             ],
             out_specs=(
                 pl.BlockSpec((rows, width), lambda b, *_: (b, 0)),
-                pl.BlockSpec((rows, context_width), lambda b, *_: (b, 0)),
+                pl.BlockSpec((rows, near), lambda b, *_: (b, 0)),
+                pl.BlockSpec((rows, far), lambda b, *_: (b, 0)),
+                pl.BlockSpec((per_step, 1, ABLK), lambda b, *_: (b, 0, 0)),
                 pl.BlockSpec((per_step, 1, ABLK), lambda b, *_: (b, 0, 0)),
             ),
             scratch_shapes=[
@@ -156,7 +182,9 @@
         cost_estimate=cost(
             10 * anchors * context_width, 4 * anchors * context_width, anchors * context_width
         ),
-    )(anchor_ids, remote_refs.reshape(-1), own_counts, table, teacher)
+    )(
+        anchor_ids, local_tiles.reshape(-1), remote_refs.reshape(-1), own_counts, table, teacher
+    )
 
 
 def take_context(block, sub, context, tiles_ref, refs_ref, table_ref, fetched_ref, counts):
@@ -181,15 +209,101 @@
 
 
 def score_kernel(
-    per_step, local_count, remote_count, slot_count, tiles_ref, refs_ref, counts_ref,
-    table_ref, fetched_ref, anchors_ref, target_ref, base_ref,
-    kl_ref, delta_ref, remote_grad_ref, remote_acc, context,
+    per_step, remote_count, slot_count, refs_ref, counts_ref,
+    fetched_ref, anchors_ref, far_ref, base_ref, partial_ref,
+    kl_ref, inverse_ref, delta_ref, remote_grad_ref, remote_acc,
 ):
-    tiles = local_count + remote_count
-
     @pl.when(pl.program_id(0) == 0)
     def _():
         clear_rows(remote_acc)
+
+    for sub in range(per_step):
+        block = pl.program_id(0) * per_step + sub
+        rows = slice(sub * ABLK, (sub + 1) * ABLK)
+        anchors = anchors_ref[rows, :]
+        places = []
+        student = []
+        student_sum = gap_sum = None
+        for i in range(remote_count):
+            span = slice(i * TILE, (i + 1) * TILE)
+            ref = refs_ref[block * remote_count + i]
+            places.append(rows_of(ref))
+            live = lax.rem(ref, slot_count) < counts_ref[lax.div(ref, slot_count)]
+            scores = tile_scores(anchors, fetched_ref[places[i], :])
+            student_exp = jnp.exp(scores) * jnp.where(live, 1.0, 0.0).astype(jnp.float32)
+            gap = far_ref[rows, span].astype(jnp.float32) * scores
+            student_sum = student_exp if i == 0 else student_sum + student_exp
+            gap_sum = gap if i == 0 else gap_sum + gap
+            student.append(student_exp)
+        total = as_column(partial_ref[sub]) + jnp.sum(student_sum, axis=1, keepdims=True)
+        inverse = 1.0 / total
+        rest = jnp.log(total) - jnp.sum(gap_sum, axis=1, keepdims=True)
+        kl_ref[sub] = base_ref[sub] + as_row(rest)
+        inverse_ref[sub] = as_row(inverse)
+        for i in range(remote_count):
+            span = slice(i * TILE, (i + 1) * TILE)
+            delta = (student[i] * inverse - far_ref[rows, span].astype(jnp.float32)).astype(
+                jnp.bfloat16
+            )
+            delta_ref[rows, span] = delta
+            remote_acc[places[i], :] += tile_grad(delta, anchors)
+
+    @pl.when(pl.program_id(0) == pl.num_programs(0) - 1)
+    def _():
+        def finish(index, carry):
+            here = rows_of(index, CHUNK)
+            remote_grad_ref[here, :] = remote_acc[here, :].astype(jnp.bfloat16)
+            return carry
+
+        lax.fori_loop(0, remote_acc.shape[0] // CHUNK, finish, 0)
+
+
+def score(per_step, remote_refs, own_counts, fetched, prepared, slots):
+    anchors, near, far, base, partial = prepared
+    blocks, remote_count = remote_refs.shape
+    width = anchors.shape[1]
+    rows = per_step * ABLK
+    pairs = far.shape[0] * far.shape[1]
+    row_spec = pl.BlockSpec((per_step, 1, ABLK), lambda b, *_: (b, 0, 0))
+    far_spec = pl.BlockSpec((rows, far.shape[1]), lambda b, *_: (b, 0))
+    return pl.pallas_call(
+        functools.partial(score_kernel, per_step, remote_count, slots),
+        out_shape=(
+            jax.ShapeDtypeStruct((blocks, 1, ABLK), jnp.float32),
+            jax.ShapeDtypeStruct((blocks, 1, ABLK), jnp.float32),
+            jax.ShapeDtypeStruct(far.shape, jnp.bfloat16),
+            jax.ShapeDtypeStruct(fetched.shape, jnp.bfloat16),
+        ),
+        grid_spec=pltpu.PrefetchScalarGridSpec(
+            num_scalar_prefetch=2,
+            grid=(blocks // per_step,),
+            in_specs=[
+                whole(fetched.shape),
+                pl.BlockSpec((rows, width), lambda b, *_: (b, 0)),
+                far_spec,
+                row_spec,
+                row_spec,
+            ],
+            out_specs=(row_spec, row_spec, far_spec, whole(fetched.shape)),
+            scratch_shapes=[pltpu.VMEM(fetched.shape, jnp.float32)],
+        ),
+        compiler_params=pltpu.CompilerParams(vmem_limit_bytes=VMEM_LIMIT),
+        cost_estimate=cost(3 * pairs * width, 4 * pairs, pairs),
+    )(remote_refs.reshape(-1), own_counts, fetched, anchors, far, base, partial)
+
+
+def local_kernel(
+    per_step, local_count, remote_count, lanes, ids_ref, tiles_ref, refs_ref,
+    table_ref, fetched_ref, anchors_ref, near_ref, inverse_ref, delta_ref, local_grad_ref,
+    context, near_delta, anchor_grad, *row_accs,
+):
+    scale = SCORE_SCALE / table_ref.shape[1]
+
+    @pl.when(pl.program_id(0) == 0)
+    def _():
+        clear_rows(local_grad_ref)
+        for acc in row_accs:
+            clear_rows(acc)
 
     for sub in range(per_step):
         block = pl.program_id(0) * per_step + sub
@@ -199,118 +313,21 @@
             (local_count, remote_count),
         )
         anchors = anchors_ref[rows, :]
-        student = []
-        student_sum = gap_sum = None
-        for i in range(tiles):
-            span = slice(i * TILE, (i + 1) * TILE)
-            scores = lax.dot_general(
-                anchors,
-                context[sub, span, :],
-                (((1,), (1,)), ((), ())),
-                preferred_element_type=jnp.float32,
-            )
-            student_exp = jnp.exp(scores)
-            if i >= local_count:
-                ref = refs_ref[block * remote_count + i - local_count]
-                live = lax.rem(ref, slot_count) < counts_ref[lax.div(ref, slot_count)]
-                student_exp = student_exp * jnp.where(live, 1.0, 0.0).astype(jnp.float32)
-            gap = target_ref[rows, span].astype(jnp.float32) * scores
-            student_sum = student_exp if i == 0 else student_sum + student_exp
-            gap_sum = gap if i == 0 else gap_sum + gap
-            student.append(student_exp)
-        total = jnp.sum(student_sum, axis=1, keepdims=True)
-        inverse = 1.0 / total
-        rest = jnp.log(total) - jnp.sum(gap_sum, axis=1, keepdims=True)
-        kl_ref[sub] = base_ref[sub] + as_row(rest)
-        for i in range(tiles):
-            span = slice(i * TILE, (i + 1) * TILE)
-            delta = (student[i] * inverse - target_ref[rows, span].astype(jnp.float32)).astype(
-                jnp.bfloat16
-            )
-            delta_ref[rows, span] = delta
-            if i >= local_count:
-                remote_acc[places[i], :] += tile_grad(delta, anchors)
-
-    @pl.when(pl.program_id(0) == pl.num_programs(0) - 1)
-    def _():
-        def finish(index, carry):
-            here = rows_of(index, CHUNK)
-            remote_grad_ref[here, :] = remote_acc[here, :].astype(jnp.bfloat16)
-            return carry
-
-        lax.fori_loop(0, remote_acc.shape[0] // CHUNK, finish, 0)
-
-
-def score(per_step, local_tiles, remote_refs, own_counts, table, fetched, prepared, slots):
-    anchors, target, base = prepared
-    blocks, local_count = local_tiles.shape
-    remote_count = remote_refs.shape[1]
-    context_width = target.shape[1]
-    width = table.shape[1]
-    rows = per_step * ABLK
-    pairs = target.shape[0] * context_width
-    return pl.pallas_call(
-        functools.partial(score_kernel, per_step, local_count, remote_count, slots),
-        out_shape=(
-            jax.ShapeDtypeStruct((blocks, 1, ABLK), jnp.float32),
-            jax.ShapeDtypeStruct(target.shape, jnp.bfloat16),
-            jax.ShapeDtypeStruct(fetched.shape, jnp.bfloat16),
-        ),
-        grid_spec=pltpu.PrefetchScalarGridSpec(
-            num_scalar_prefetch=3,
-            grid=(blocks // per_step,),
-            in_specs=[
-                whole(table.shape),
-                whole(fetched.shape),
-                pl.BlockSpec((rows, width), lambda b, *_: (b, 0)),
-                pl.BlockSpec((rows, context_width), lambda b, *_: (b, 0)),
-                pl.BlockSpec((per_step, 1, ABLK), lambda b, *_: (b, 0, 0)),
-            ],
-            out_specs=(
-                pl.BlockSpec((per_step, 1, ABLK), lambda b, *_: (b, 0, 0)),
-                pl.BlockSpec((rows, context_width), lambda b, *_: (b, 0)),
-                whole(fetched.shape),
-            ),
-            scratch_shapes=[
-                pltpu.VMEM(fetched.shape, jnp.float32),
-                pltpu.VMEM((per_step, context_width, width), jnp.bfloat16),
-            ],
-        ),
-        compiler_params=pltpu.CompilerParams(vmem_limit_bytes=VMEM_LIMIT),
-        cost_estimate=cost(3 * pairs * width, 4 * pairs, pairs),
-    )(
-        local_tiles.reshape(-1), remote_refs.reshape(-1), own_counts,
-        table, fetched, anchors, target, base,
-    )
-
-
-def local_kernel(
-    per_step, local_count, remote_count, lanes, ids_ref, tiles_ref, refs_ref,
-    table_ref, fetched_ref, anchors_ref, delta_ref, local_grad_ref,
-    context, anchor_grad, *row_accs,
-):
-    scale = SCORE_SCALE / table_ref.shape[1]
-
-    @pl.when(pl.program_id(0) == 0)
-    def _():
-        clear_rows(local_grad_ref)
-        for acc in row_accs:
-            clear_rows(acc)
-
-    for sub in range(per_step):
-        block = pl.program_id(0) * per_step + sub
-        rows = slice(sub * ABLK, (sub + 1) * ABLK)
-        places = take_context(
-            block, sub, context, tiles_ref, refs_ref, table_ref, fetched_ref,
-            (local_count, remote_count),
-        )
-        anchor_grad[rows, :] = (
-            jnp.dot(delta_ref[rows, :], context[sub], preferred_element_type=jnp.float32) * scale
-        )
-        anchors = anchors_ref[rows, :]
+        inverse = as_column(inverse_ref[sub])
+        near = local_count * TILE
         for i in range(local_count):
             span = slice(i * TILE, (i + 1) * TILE)
-            local_grad_ref[places[i], :] += tile_grad(delta_ref[rows, span], anchors)
+            student = jnp.exp(tile_scores(anchors, context[sub, span, :])) * inverse
+            delta = (student - near_ref[rows, span].astype(jnp.float32)).astype(jnp.bfloat16)
+            near_delta[rows, span] = delta
+            local_grad_ref[places[i], :] += tile_grad(delta, anchors)
+        near_part = jnp.dot(
+            near_delta[rows, :], context[sub, :near, :], preferred_element_type=jnp.float32
+        )
+        far_part = jnp.dot(
+            delta_ref[rows, :], context[sub, near:, :], preferred_element_type=jnp.float32
+        )
+        anchor_grad[rows, :] = (near_part + far_part) * scale
         for row in range(ABLK):
             acc = row_accs[row % lanes]
             at = sub * ABLK + row
@@ -329,10 +346,12 @@
         lax.fori_loop(0, local_grad_ref.shape[0] // CHUNK, finish, 0)
 
 
-def local_grads(per_step, anchor_ids, local_tiles, remote_refs, table, fetched, anchors, delta):
+def local_grads(
+    per_step, anchor_ids, local_tiles, remote_refs, table, fetched, anchors, near, inverse, delta
+):
     blocks, local_count = local_tiles.shape
     remote_count = remote_refs.shape[1]
-    context_width = delta.shape[1]
+    context_width = near.shape[1] + delta.shape[1]
     width = table.shape[1]
     rows = per_step * ABLK
     lanes = 4 if table.shape[0] <= 8192 else 1
@@ -347,11 +366,14 @@
                 whole(table.shape),
                 whole(fetched.shape),
                 pl.BlockSpec((rows, width), lambda b, *_: (b, 0)),
-                pl.BlockSpec((rows, context_width), lambda b, *_: (b, 0)),
+                pl.BlockSpec((rows, near.shape[1]), lambda b, *_: (b, 0)),
+                pl.BlockSpec((per_step, 1, ABLK), lambda b, *_: (b, 0, 0)),
+                pl.BlockSpec((rows, delta.shape[1]), lambda b, *_: (b, 0)),
             ],
             out_specs=whole(table.shape),
             scratch_shapes=[
                 pltpu.VMEM((per_step, context_width, width), jnp.bfloat16),
+                pltpu.VMEM((rows, near.shape[1]), jnp.bfloat16),
                 pltpu.VMEM((rows, width), jnp.float32),
             ]
             + [pltpu.VMEM(table.shape, jnp.float32)] * lanes,
@@ -360,7 +382,7 @@
         cost_estimate=cost(3 * pairs * width, 2 * pairs, 0),
     )(
         anchor_ids, local_tiles.reshape(-1), remote_refs.reshape(-1),
-        table, fetched, anchors, delta,
+        table, fetched, anchors, near, inverse, delta,
     )
 
 
@@ -654,16 +676,16 @@
     fetched = lax.all_to_all(served, "group", split_axis=0, concat_axis=0, tiled=True)
     per_step = math.gcd(local_tiles.shape[0], 2)
     prepared = prepare(
-        per_step, anchor_ids, remote_refs, local_tiles.shape[1], own_counts, table, teacher,
-        slot_count,
-    )
-    anchor_kl, delta, remote_grad = score(
-        per_step, local_tiles, remote_refs, own_counts, table, fetched, prepared, slot_count
+        per_step, anchor_ids, local_tiles, remote_refs, own_counts, table, teacher, slot_count
+    )
+    anchor_kl, inverse, delta, remote_grad = score(
+        per_step, remote_refs, own_counts, fetched, prepared, slot_count
     )
     anchor_kl = anchor_kl.reshape(-1)
     returned = lax.all_to_all(remote_grad, "group", split_axis=0, concat_axis=0, tiled=True)
     local_grad = local_grads(
-        per_step, anchor_ids, local_tiles, remote_refs, table, fetched, prepared[0], delta
+        per_step, anchor_ids, local_tiles, remote_refs, table, fetched, prepared[0], prepared[1],
+        inverse, delta,
     )
     merged = merge(asked, local_grad, returned)
     node_grad = scatter_sums(merged, doms)

time: 248 us -> 247 us (level)
  Pallas kernels: 144 us -> 166 us
  waiting for transfers between devices: 55.7 us -> 34.4 us
    pallas_call x1, Pallas kernels: 20.9 us -> 40.1 us  [local_grads(): pl.pallas_call(functools.partial(local_kernel, per_step, local_count, rem...]
    all_to_all x1, waiting for transfers between devices: 26.6 us -> 7.46 us  [shards(): lax.all_to_all(remote_grad, 'group', split_axis=0, concat_axis=0, tiled=T...]
  transfers between devices with their start and end apart: 2 -> 2, of which waited for: 2 -> 2; matrix products, arithmetic and copies ran while one was open for 1% -> 1% of each run, Pallas kernels for 15% -> 24%
where the time goes in v4:
time: 247 us; the launch traced here: 246 us
  Pallas kernels  166 us (67%)
  waiting for transfers between devices  34.4 us (14%)
  matrix products  15.8 us (6%)
  local copies, waits for them, and re-layouts  14.7 us (6%)
  starting transfers between devices  8.28 us (3%)
  other arithmetic  6.43 us (3%)
    pallas_call x1, Pallas kernels, local_grads(): pl.pallas_call(functools.partial(local_kernel, per_step, local_count, rem...  40.1 us
    pallas_call x1, Pallas kernels, mean_over_devices(): pl.pallas_call(functools.partial(totals_kernel, groups, doms), out_shape=...  30.3 us
    all_to_all x1, waiting for transfers between devices, shards(): lax.all_to_all(served, 'group', split_axis=0, concat_axis=0, tiled=True)  27 us
    pallas_call x1, Pallas kernels, score(): pl.pallas_call(functools.partial(score_kernel, per_step, remote_count, sl...  25.1 us
    pallas_call x1, Pallas kernels, gather_table(): pl.pallas_call(functools.partial(gather_kernel, groups, doms), out_shape=...  22.4 us
    pallas_call x1, Pallas kernels, prepare(): pl.pallas_call(functools.partial(prepare_kernel, per_step, local_count, r...  18.9 us
    pallas_call x1, Pallas kernels, scatter_sums(): pl.pallas_call(functools.partial(scatter_kernel, doms), out_shape=jax.Sha...  18.6 us
    unnamed x30, local copies, waits for them, and re-layouts  7.8 us
  transfers between devices with their start and end apart: 2, of which 2 were waited for; matrix products, arithmetic and copies ran while one was open for 1% of the time, Pallas kernels for 24%

profile of v4, /device:TPU:1, one launch (start us, length us, event | category | flops | bytes accessed | tf_op | source)
XLA Modules:
  0.0 246.2 jit_solution(3147456444425105635)
XLA Ops:
  0.6 0.0 copy-start
  0.6 0.0 copy-start.8
  0.7 1.0 copy-done
  1.7 5.3 %multiply_convert_fusion = (bf16[2048,1024]{1,0:T(8,128)(2,1)S(1)}, f32[2048,1024]{1,0:T(8,128)}) fusion(f32[1024]{0:T(1024)} %param.12, bf16[2048,128]{1,0:T(8,128)(2,1)S(1)} %copy-done, bf16[128,1024]{1,0:T(8,128)(2,1)} %param.11), kind=kOutput, calls=%fused_computation.1 | convolution fusion | flops 549453824 | bytes 13373440 | tf_op jit(solution)/shard_map/dot_general | solution.py:27
  7.0 2.0 copy-done.1
  9.0 0.0 copy-done.8
  9.0 1.5 multiply_reduce_fusion.1
  10.5 0.3 copy.20
  10.8 0.0 copy-start.5
  10.9 1.2 fusion.2.unit_ref
  12.0 0.0 copy-done.9
  12.0 0.6 pad.4.requests_ref
  12.7 22.4 %shard_map.137 = (bf16[8192,128]{1,0:T(8,128)(2,1)}, s32[8,8,128]{2,1,0:T(8,128)}) custom-call(bf16[2048,128]{1,0:T(8,128)(2,1)} %fusion.2.unit_ref, s32[8,8,128]{2,1,0:T(8,128)} %pad.4.requests_ref), custom_call_target="tpu_custom_call" | custom-call | tf_op jit(solution)/shard_map/pallas_call | solution.py:504
  35.1 0.8 slice_reduce_fusion
  35.9 0.6 reshape_squeeze.3.asked_ref
  36.5 4.0 %shard_map.138 = bf16[8192,128]{1,0:T(8,128)(2,1)} custom-call(s32[64]{0:T(128)} %reshape_squeeze.3.asked_ref, bf16[8192,128]{1,0:T(8,128)(2,1)} %get-tuple-element.17.table_ref), custom_call_target="tpu_custom_call" | custom-call | tf_op jit(solution)/shard_map/pallas_call | solution.py:49
  40.5 0.0 copy-done.5
  40.5 3.6 %all-to-all-start = ((bf16[8,1024,128]{2,1,0:T(8,128)(2,1)}), bf16[8,1024,128]{2,1,0:T(8,128)(2,1)S(1)}, u32[]{:S(2)}, u32[]{:S(2)}) async-start(bf16[8,1024,128]{2,1,0:T(8,128)(2,1)} %bitcast.25), calls=%async_computation | async-start | bytes 4194304 | tf_op jit(solution)/shard_map/all_to_all | solution.py:676
  44.1 0.0 copy-done.10
  44.1 0.1 copy.19
  44.2 0.6 reshape.49.refs_ref
  44.8 0.1 copy.21
  44.9 0.6 reshape.50.tiles_ref
  45.5 18.9 %shard_map.139 = (bf16[4096,128]{1,0:T(8,128)(2,1)}, bf16[4096,512]{1,0:T(8,128)(2,1)}, bf16[4096,512]{1,0:T(8,128)(2,1)}, f32[32,1,128]{2,1,0:T(1,128)}, f32[32,1,128]{2,1,0:T(1,128)}) custom-call(s32[4096]{0:T(1024)} %ids_ref.3, s32[128]{0:T(128)} %reshape.50.tiles_ref, s32[128]{0:T(128)} %reshape.49.refs_ref, s32[8]{0:T(128)} %bitcast.32, ...), custom_call_target="tpu_custom_call" | custom-call | flops 41943040 | bytes 16777216 | tf_op jit(solution)/shard_map/pallas_call | solution.py:153
  64.4 27.0 %all-to-all-done = bf16[8,1024,128]{2,1,0:T(8,128)(2,1)S(1)} async-done(((bf16[8,1024,128]{2,1,0:T(8,128)(2,1)}), bf16[8,1024,128]{2,1,0:T(8,128)(2,1)S(1)}, u32[]{:S(2)}, u32[]{:S(2)}) %all-to-all-start) | async-done | bytes 2097184 | tf_op jit(solution)/shard_map/all_to_all | solution.py:676
  91.4 1.3 copy-done.3
  92.7 25.1 %shard_map.140 = (f32[32,1,128]{2,1,0:T(1,128)}, f32[32,1,128]{2,1,0:T(1,128)}, bf16[4096,512]{1,0:T(8,128)(2,1)}, bf16[8192,128]{1,0:T(8,128)(2,1)}) custom-call(s32[128]{0:T(128)} %reshape.49.refs_ref, s32[8]{0:T(128)} %bitcast.33, bf16[8192,128]{1,0:T(8,128)(2,1)} %bitcast.23, bf16[4096,128]{1,0:T(8,128)(2,1)} %get-tuple-element.18.anchors_ref, ...), custom_call_target="tpu_custom_call" | custom-call | flops 805306368 | bytes 8388608 | tf_op jit(solution)/shard_map/pallas_call | solution.py:269
  117.8 4.7 %all-to-all-start.1 = ((bf16[8,1024,128]{2,1,0:T(8,128)(2,1)}), bf16[8,1024,128]{2,1,0:T(8,128)(2,1)S(1)}, u32[]{:S(2)}, u32[]{:S(2)}) async-start(bf16[8,1024,128]{2,1,0:T(8,128)(2,1)} %bitcast.29), calls=%async_computation.1 | async-start | bytes 4194304 | tf_op jit(solution)/shard_map/all_to_all | solution.py:685
  122.5 0.1 pad.8.clone
  122.5 40.1 %shard_map.141.local_ref = f32[8192,128]{1,0:T(8,128)} custom-call(s32[4096]{0:T(1024)} %ids_ref.3, s32[128]{0:T(128)} %reshape.50.tiles_ref, s32[128]{0:T(128)} %reshape.49.refs_ref, bf16[8192,128]{1,0:T(8,128)(2,1)} %get-tuple-element.17.table_ref, bf16[8192,128]{1,0:T(8,128)(2,1)} %bitcast.24, bf16[4096,128]{1,0:T(8,128)(2,1)} %get-tuple-element.18.anchors_ref, ...), custom_call_target="tpu_custom_call" | custom-call | flops 1610612736 | bytes 8388608 | tf_op jit(solution)/shard_map/pallas_call | solution.py:359
  162.6 7.5 %all-to-all-done.1 = bf16[8,1024,128]{2,1,0:T(8,128)(2,1)S(1)} async-done(((bf16[8,1024,128]{2,1,0:T(8,128)(2,1)}), bf16[8,1024,128]{2,1,0:T(8,128)(2,1)S(1)}, u32[]{:S(2)}, u32[]{:S(2)}) %all-to-all-start.1) | async-done | bytes 2097184 | tf_op jit(solution)/shard_map/all_to_all | solution.py:685
  170.1 1.3 copy-done.7
  171.4 6.3 %shard_map.142.merged_ref = bf16[8192,128]{1,0:T(8,128)(2,1)} custom-call(s32[64]{0:T(128)} %reshape_squeeze.3.asked_ref, f32[8192,128]{1,0:T(8,128)} %shard_map.141.local_ref, bf16[8192,128]{1,0:T(8,128)(2,1)} %bitcast.26), custom_call_target="tpu_custom_call" | custom-call | tf_op jit(solution)/shard_map/pallas_call | solution.py:412
  177.7 18.6 %shard_map.143 = f32[2048,128]{1,0:T(8,128)} custom-call(bf16[8192,128]{1,0:T(8,128)(2,1)} %shard_map.142.merged_ref), custom_call_target="tpu_custom_call" | custom-call | tf_op jit(solution)/shard_map/pallas_call | solution.py:565
  196.4 0.0 copy-done.6
  196.4 0.0 copy-start.2
  196.4 2.0 multiply_reduce_fusion
  198.4 0.0 copy-start.12
  198.4 1.8 divide_convert_fusion
  200.2 1.3 fusion.5
  201.5 6.4 %fusion.4 = (f32[1024]{0:T(1024)S(1)}, bf16[2048,1024]{1,0:T(8,128)(2,1)S(1)}) fusion(f32[2048,1024]{1,0:T(8,128)} %get-tuple-element.40, f32[1024]{0:T(1024)S(1)} %copy-done.12, bf16[2048,128]{1,0:T(8,128)(2,1)S(1)} %divide_convert_fusion, bf16[1024,128]{1,0:T(8,128)(2,1)S(1)} %copy-done.8), kind=kOutput, calls=%fused_computation.17 | convolution fusion | flops 559938560 | bytes 13377536 | tf_op jit(solution)/shard_map/dot_general | solution.py:697
  207.9 1.3 fusion
  209.2 1.5 maximum_maximum_fusion.x_ref
  210.7 30.3 %shard_map.144 = f32[4,8,80,128]{3,2,1,0:T(8,128)} custom-call(f32[2560,128]{1,0:T(8,128)} %maximum_maximum_fusion.x_ref), custom_call_target="tpu_custom_call" | custom-call | tf_op jit(solution)/shard_map/pallas_call | solution.py:642
  240.9 2.1 fusion.3
  243.0 1.3 slice_bitcast_fusion.1
  244.3 1.0 copy.22
  245.3 1.0 copy.24
  (16 shorter events, 0.0 us)
Async XLA Ops:
  0.6 1.0 copy-start
  0.6 8.3 %copy-start.8 = (bf16[1024,128]{1,0:T(8,128)(2,1)S(1)}, bf16[1024,128]{1,0:T(8,128)(2,1)}, u32[]{:S(2)}) copy-start(bf16[1024,128]{1,0:T(8,128)(2,1)} %param.13) | copy-start | bytes 786436
  7.0 2.0 copy-start.1
  9.0 3.1 %copy-start.9 = (s32[1,1,8,8]{3,2,1,0:T(8,128)S(1)}, s32[1,1,8,8]{3,2,1,0:T(8,128)}, u32[]{:S(2)}) copy-start(s32[1,1,8,8]{3,2,1,0:T(8,128)} %param.16) | copy-start | bytes 772
  10.8 29.6 %copy-start.5 = (f32[2048,128]{1,0:T(8,128)}, f32[2048,128]{1,0:T(8,128)S(1)}, u32[]{:S(2)}) copy-start(f32[2048,128]{1,0:T(8,128)S(1)} %copy.20) | copy-start | bytes 3145732
  36.5 7.6 %copy-start.10 = (s32[32,4]{0,1:T(4,128)S(1)}, s32[32,4]{0,1:T(4,128)}, u32[]{:S(2)}) copy-start(s32[32,4]{0,1:T(4,128)} %param.18) | copy-start | bytes 1540
  36.5 8.3 %copy-start.11 = (s32[32,4]{0,1:T(4,128)S(1)}, s32[32,4]{0,1:T(4,128)}, u32[]{:S(2)}) copy-start(s32[32,4]{0,1:T(4,128)} %param.15) | copy-start | bytes 1540
  40.5 50.9 %all-to-all-start = ((bf16[8,1024,128]{2,1,0:T(8,128)(2,1)}), bf16[8,1024,128]{2,1,0:T(8,128)(2,1)S(1)}, u32[]{:S(2)}, u32[]{:S(2)}) async-start(bf16[8,1024,128]{2,1,0:T(8,128)(2,1)} %bitcast.25), calls=%async_computation | async-start | bytes 4194304 | tf_op jit(solution)/shard_map/all_to_all | solution.py:676
  91.4 1.3 copy-start.3
  117.8 52.3 %all-to-all-start.1 = ((bf16[8,1024,128]{2,1,0:T(8,128)(2,1)}), bf16[8,1024,128]{2,1,0:T(8,128)(2,1)S(1)}, u32[]{:S(2)}, u32[]{:S(2)}) async-start(bf16[8,1024,128]{2,1,0:T(8,128)(2,1)} %bitcast.29), calls=%async_computation.1 | async-start | bytes 4194304 | tf_op jit(solution)/shard_map/all_to_all | solution.py:685
  170.1 1.3 copy-start.7
  171.4 25.0 %copy-start.6 = (f32[2048,128]{1,0:T(8,128)S(1)}, f32[2048,128]{1,0:T(8,128)}, u32[]{:S(2)}) copy-start(f32[2048,128]{1,0:T(8,128)} %copy-done.5) | copy-start | bytes 3145732
  196.4 3.8 %copy-start.2 = (bf16[2048,1024]{1,0:T(8,128)(2,1)S(1)}, bf16[2048,1024]{1,0:T(8,128)(2,1)}, u32[]{:S(2)}) copy-start(bf16[2048,1024]{1,0:T(8,128)(2,1)} %copy-done.1) | copy-start | bytes 12582916
  198.4 3.1 %copy-start.12 = (f32[1024]{0:T(1024)S(1)}, f32[1024]{0:T(1024)}, u32[]{:S(2)}) copy-start(f32[1024]{0:T(1024)} %param.12) | copy-start | bytes 12292
  209.2 36.1 %copy-start.4 = (f32[2048,128]{1,0:T(8,128)S(1)}, f32[2048,128]{1,0:T(8,128)}, u32[]{:S(2)}) copy-start(f32[2048,128]{1,0:T(8,128)} %shard_map.143) | copy-start | bytes 3145732
